TPU v7x, 512 devices: a whole 4x8x8 slice. The times are simulated.
512 devices in a mesh: grp: 2 (over z_lo), gx: 32 (over y, z_hi), gy: 8 (over x, core).
Axes of the slice: x: 4, y: 8, z: 8 (z_hi: 4, z_lo: 2; z = z_hi * 2 + z_lo), core: 2. Of those that a mesh axis runs over, the one named last changes fastest.
Arguments:
- flow_state: float32 [2, 4, 512, 64, 128], P('grp', None, 'gx', 'gy'), may hold values from -6 to 6
- block_offset: int32 [128], P('gx'), may hold values from -3 to 3, as said below
- block_weight: float32 [128], P('gx'), may hold values from 0.1 to 0.9
Outputs:
- advanced: float32 [2, 4, 512, 64, 128], P('grp', None, 'gx', 'gy')
Inputs may be any that keep to these rules, and one draw needn't show every extreme that they name: Block b's lamb reaches blocks b + block_offset[b] and the next one, counted modulo 128; in every brick of 4 blocks the first block has a negative offset and the last block an offset of 0 or more.
All inputs are finite; a program needn't handle non-finite values.
Results may differ from a plain program's by a relative error of at most 0.00005.
Values sent between devices are 32-bit elements; how exact they have to be, the bound alone decides.
A program may use at most 64 MiB of HBM per device.

v0:
```python
import jax
import jax.numpy as jnp
from jax import lax
from jax.sharding import PartitionSpec as P

drp_weights = (
    0.907646591371,
    -0.337048393268,
    0.133442885327,
    -0.045246480208,
    0.011169294114,
    -0.001456501759,
)
viscosity = 0.05
mean_flow = 0.5
les_time_step = 0.1
ape_time_step = 0.4


def extended_2(shard, sides, width):
    edges = {}
    for axis, dim in sides:
        size, length = (lax.axis_size(axis), shard.shape[dim])
        up = [(i, (i + 1) % size) for i in range(size)]
        last = lax.slice_in_dim(shard, length - width, length, axis=dim)
        first = lax.slice_in_dim(shard, 0, width, axis=dim)
        edges[dim] = (
            lax.ppermute(last, axis, up),
            lax.ppermute(first, axis, [(b, a) for a, b in up]),
        )
    done = []
    for _, dim in sides:
        low, high = edges[dim]
        around = [(width, width) if d in done else (0, 0) for d in range(shard.ndim)]
        shard = jnp.concatenate([jnp.pad(low, around), shard, jnp.pad(high, around)], axis=dim)
        done.append(dim)
    return shard


def from_behind(block, axis, distance):
    devices = range(lax.axis_size(axis))
    route = [((i - distance) % len(devices), i) for i in devices]
    return lax.ppermute(block, axis, route)


def passed_along(block, axis, distance):
    devices = range(lax.axis_size(axis))
    route = [(i - distance, i) for i in devices if i - distance in devices]
    return lax.ppermute(block, axis, route)


def shifted(extended, margin, direction, offset_j):
    width_x = extended.shape[1] - 2 * margin
    width_y = extended.shape[2] - 2 * margin
    if direction == 1:
        return extended[
            :, margin + offset_j : margin + offset_j + width_x, margin : margin + width_y
        ]
    if direction == 2:
        return extended[
            :, margin : margin + width_x, margin + offset_j : margin + offset_j + width_y
        ]
    centre = extended[:, margin : margin + width_x, margin : margin + width_y]
    return jnp.roll(centre, -offset_j, axis=3)


def derivative(extended, margin, weight_list, direction):
    total = None
    for offset_j, weight_j in enumerate(weight_list, start=1):
        term = weight_j * (
            shifted(extended, margin, direction, offset_j)
            - shifted(extended, margin, direction, -offset_j)
        )
        total = term if total is None else total + term
    return total


def les_tendency(extended, margin):
    grad_x, grad_y, grad_z = [
        derivative(extended, margin, (0.5,), direction) for direction in (1, 2, 3)
    ]
    centre = shifted(extended, margin, 1, 0)
    vel_x, vel_y, vel_z = (centre[0], centre[1], centre[2])
    vort_x = grad_y[2] - grad_z[1]
    vort_y = grad_z[0] - grad_x[2]
    vort_z = grad_x[1] - grad_y[0]
    lamb_vec = jnp.stack(
        [
            vort_y * vel_z - vort_z * vel_y,
            vort_z * vel_x - vort_x * vel_z,
            vort_x * vel_y - vort_y * vel_x,
        ]
    )
    spread = -6.0 * centre
    for direction in (1, 2, 3):
        spread = (
            spread
            + shifted(extended, margin, direction, 1)
            + shifted(extended, margin, direction, -1)
        )
    tend_vel = -lamb_vec + viscosity * spread[:3]
    tend_scalar = (
        -(vel_x * grad_x[3] + vel_y * grad_y[3] + vel_z * grad_z[3]) + viscosity * spread[3]
    )
    return (jnp.concatenate([tend_vel, tend_scalar[None]], axis=0), lamb_vec)


def ape_tendency(extended, margin, source):
    grad_x, grad_y, grad_z = [
        derivative(extended, margin, drp_weights, direction) for direction in (1, 2, 3)
    ]
    tend_press = -mean_flow * grad_x[0] - (grad_x[1] + grad_y[2] + grad_z[3])
    tend_vel = -mean_flow * grad_x[1:] - jnp.stack([grad_x[0], grad_y[0], grad_z[0]]) - source
    return jnp.concatenate([tend_press[None], tend_vel], axis=0)


def walls(extended, margin):
    local_rows = extended.shape[2] - 2 * margin
    row_index = (
        jnp.arange(extended.shape[2], dtype=jnp.int32) + lax.axis_index("gy") * local_rows - margin
    )
    inside = (row_index >= 0) & (row_index < local_rows * lax.axis_size("gy"))
    return extended * inside[None, None, :, None].astype(extended.dtype)


def tendencies(fields, is_les, block_offset, block_weight):
    wide = walls(extended_2(fields, (("gx", 1), ("gy", 2)), 6), 6)
    les_ext, les_margin, ape_ext = (wide, 6, wide)

    def les_branch():
        return les_tendency(les_ext, les_margin)

    def spare_branch():
        return (jnp.zeros_like(fields), jnp.zeros((3,) + fields.shape[1:], fields.dtype))

    les_part, lamb_vec = lax.cond(is_les, les_branch, spare_branch)
    local_blocks = block_offset.shape[0]
    blocks = lamb_vec.reshape(3, local_blocks, -1)
    target = jnp.arange(local_blocks, dtype=jnp.int32) + local_blocks + block_offset
    columns = jnp.arange(3 * local_blocks, dtype=jnp.int32)
    matrix = jnp.where(columns[None, :] == target[:, None], block_weight[:, None], 0.0)
    matrix = matrix + jnp.where(
        columns[None, :] == target[:, None] + 1, 1.0 - block_weight[:, None], 0.0
    )
    buffer = jnp.einsum("bs,cbk->csk", matrix, blocks, precision=lax.Precision.HIGHEST)
    from_next = from_behind(buffer[:, :local_blocks], "gx", -1)
    from_prev = from_behind(buffer[:, 2 * local_blocks :], "gx", 1)
    summed = buffer[:, local_blocks : 2 * local_blocks] + from_next + from_prev
    source = passed_along(summed, "grp", 1)
    source = source.reshape(lamb_vec.shape)

    def ape_branch():
        return ape_tendency(ape_ext, 6, source)

    def quiet_branch():
        return jnp.zeros_like(fields)

    ape_part = lax.cond(is_les, quiet_branch, ape_branch)
    return les_part + ape_part


def on_device(flow_state, block_offset, block_weight):
    fields = flow_state[0]
    is_les = lax.axis_index("grp") == 0
    time_step = jnp.where(is_les, les_time_step, ape_time_step).astype(fields.dtype)
    predicted = fields + time_step * tendencies(fields, is_les, block_offset, block_weight)
    corrected = predicted + time_step * tendencies(predicted, is_les, block_offset, block_weight)
    return (0.5 * (fields + corrected))[None]


def solution(mesh):
    placed = (P("grp", None, "gx", "gy", None), P("gx"), P("gx"))
    return jax.shard_map(
        on_device,
        mesh=mesh,
        in_specs=placed,
        out_specs=P("grp", None, "gx", "gy", None),
        check_vma=False,
    )
```

profile of v0, /device:TPU:64, one launch (start us, length us, event | category | flops | bytes accessed | tf_op | source)
XLA Modules:
  0.0 108.0 jit_solution(13974538479176751668)
XLA Ops:
  0.0 1.1 %fusion.89 = (f32[4,16,6,128]{3,2,1,0:T(8,128)S(1)}, f32[4,16,6,128]{3,2,1,0:T(8,128)S(1)}) fusion(f32[4,16,8,128]{3,2,1,0:T(8,128)} %bitcast.20), kind=kLoop, calls=%fused_computation.170 | loop fusion | bytes 786432 | tf_op jit(solution)/shard_map/slice | solution.py:25
  1.2 2.9 %collective-permute-start.3 = (f32[4,16,6,128]{3,2,1,0:T(8,128)S(1)}, f32[4,16,6,128]{3,2,1,0:T(8,128)S(1)}, u32[]{:S(2)}, u32[]{:S(2)}) collective-permute-start(f32[4,16,6,128]{3,2,1,0:T(8,128)S(1)} %get-tuple-element.130), channel_id=1, source_target_pairs={{1,0},{2,1},{3,2},{4,3},{5,4},{6,5},{7,6},{0,7},{9,8},{10,9},{11,1... | collective-permute-start | bytes 589832 | tf_op jit(solution)/shard_map/ppermute | solution.py:29
  4.1 1.0 fusion.88
  5.1 6.1 %collective-permute-start.1 = (f32[4,6,8,128]{3,2,1,0:T(8,128)S(1)}, f32[4,6,8,128]{3,2,1,0:T(8,128)S(1)}, u32[]{:S(2)}, u32[]{:S(2)}) collective-permute-start(f32[4,6,8,128]{3,2,1,0:T(8,128)S(1)} %get-tuple-element.127), channel_id=1, source_target_pairs={{0,8},{8,16},{16,24},{24,32},{32,40},{40,48},{48,56},{56,64},{64,7... | collective-permute-start | bytes 294920 | tf_op jit(solution)/shard_map/ppermute | solution.py:28
  11.2 8.8 %collective-permute-start.2 = (f32[4,6,8,128]{3,2,1,0:T(8,128)S(1)}, f32[4,6,8,128]{3,2,1,0:T(8,128)S(1)}, u32[]{:S(2)}, u32[]{:S(2)}) collective-permute-start(f32[4,6,8,128]{3,2,1,0:T(8,128)S(1)} %get-tuple-element.128), channel_id=1, source_target_pairs={{8,0},{16,8},{24,16},{32,24},{40,32},{48,40},{56,48},{64,56},{72,6... | collective-permute-start | bytes 294920 | tf_op jit(solution)/shard_map/ppermute | solution.py:29
  20.0 1.3 %collective-permute-done.1 = f32[4,6,8,128]{3,2,1,0:T(8,128)S(1)} collective-permute-done((f32[4,6,8,128]{3,2,1,0:T(8,128)S(1)}, f32[4,6,8,128]{3,2,1,0:T(8,128)S(1)}, u32[]{:S(2)}, u32[]{:S(2)}) %collective-permute-start.1) | collective-permute-done | bytes 98336 | tf_op jit(solution)/shard_map/ppermute | solution.py:28
  21.4 0.8 collective-permute-done.2
  22.1 0.2 fusion.39
  22.5 0.9 convolution_bitcast_fusion.1
  23.4 8.7 %collective-permute-start.4 = (f32[3,4,4096]{2,1,0:T(4,128)S(1)}, f32[3,4,4096]{2,1,0:T(4,128)S(1)}, u32[]{:S(2)}, u32[]{:S(2)}) collective-permute-start(f32[3,4,4096]{2,1,0:T(4,128)S(1)} %get-tuple-element.121), channel_id=1, source_target_pairs={{8,0},{16,8},{24,16},{32,24},{40,32},{48,40},{56,48},{64,56},{72,6... | collective-permute-start | bytes 589832 | tf_op jit(solution)/shard_map/ppermute | solution.py:43
  32.1 1.9 %collective-permute-start.5 = (f32[3,4,4096]{2,1,0:T(4,128)S(1)}, f32[3,4,4096]{2,1,0:T(4,128)S(1)}, u32[]{:S(2)}, u32[]{:S(2)}) collective-permute-start(f32[3,4,4096]{2,1,0:T(4,128)S(1)} %get-tuple-element.122), channel_id=1, source_target_pairs={{248,0},{0,8},{8,16},{16,24},{24,32},{32,40},{40,48},{48,56},{56,6... | collective-permute-start | bytes 589832 | tf_op jit(solution)/shard_map/ppermute | solution.py:43
  34.0 1.2 %collective-permute-done.4 = f32[3,4,4096]{2,1,0:T(4,128)S(1)} collective-permute-done((f32[3,4,4096]{2,1,0:T(4,128)S(1)}, f32[3,4,4096]{2,1,0:T(4,128)S(1)}, u32[]{:S(2)}, u32[]{:S(2)}) %collective-permute-start.4) | collective-permute-done | bytes 196640 | tf_op jit(solution)/shard_map/ppermute | solution.py:43
  35.3 10.3 %collective-permute-done.5 = f32[3,4,4096]{2,1,0:T(4,128)S(1)} collective-permute-done((f32[3,4,4096]{2,1,0:T(4,128)S(1)}, f32[3,4,4096]{2,1,0:T(4,128)S(1)}, u32[]{:S(2)}, u32[]{:S(2)}) %collective-permute-start.5) | collective-permute-done | bytes 196640 | tf_op jit(solution)/shard_map/ppermute | solution.py:43
  45.5 0.1 fusion.41
  45.6 1.3 %collective-permute-start.6 = (f32[3,4,4096]{2,1,0:T(4,128)S(1)}, f32[3,4,4096]{2,1,0:T(4,128)S(1)}, u32[]{:S(2)}, u32[]{:S(2)}) collective-permute-start(f32[3,4,4096]{2,1,0:T(4,128)S(1)} %fusion.41), channel_id=1, source_target_pairs={{0,256},{1,257},{2,258},{3,259},{4,260},{5,261},{6,262},{7,263},{8... | collective-permute-start | bytes 589832 | tf_op jit(solution)/shard_map/ppermute | solution.py:49
  46.9 6.3 %collective-permute-done.6 = f32[3,4,4096]{2,1,0:T(4,128)S(1)} collective-permute-done((f32[3,4,4096]{2,1,0:T(4,128)S(1)}, f32[3,4,4096]{2,1,0:T(4,128)S(1)}, u32[]{:S(2)}, u32[]{:S(2)}) %collective-permute-start.6) | collective-permute-done | bytes 196640 | tf_op jit(solution)/shard_map/ppermute | solution.py:49
  53.2 3.9 %conditional.5 = (f32[4,16,8,128]{3,2,1,0:T(8,128)S(1)}) conditional(s32[]{:T(128)} %convert_element_type.20, (f32[4,28,20,128]{3,2,1,0:T(8,128)S(1)}, f32[3,4,4096]{2,1,0:T(4,128)S(1)}) %tuple.38, () %tuple.39), branch_computations={%region_2.3_spmd, %region_3.4_spmd} | conditional | flops 4505600 | bytes 18874376 | solution.py:158
  53.2 0.1 fusion.58
  53.3 0.1 fusion.59
  53.5 0.1 fusion.60
  53.6 0.1 fusion.61
  53.8 0.1 fusion.62
  53.9 0.1 fusion.63
  54.0 0.1 fusion.64
  54.2 0.1 fusion.65
  54.3 0.1 fusion.66
  54.5 0.1 fusion.67
  54.6 0.1 fusion.68
  54.7 0.1 fusion.69
  54.9 1.4 %fusion.10 = f32[4,16,8,128]{3,2,1,0:T(8,128)S(1)} fusion(f32[4,16,8,1]{3,2,1,0:T(8,128)S(1)} %get-tuple-element.71, f32[4,16,8,127]{3,2,1,0:T(8,128)S(1)} %get-tuple-element.73, f32[4,16,8,127]{3,2,1,0:T(8,128)S(1)} %get-tuple-element.72, f32[4,16,8,1]{3,2,1,0:T(8,128)S(1)} %get-tuple-element.70, f32[4,16,8,2]{3,2,1,0:T(8,128)S(1)} %get-tuple-element.67, ...), kind=kLoop, calls=%fused_computation.30 | loop fusion | flops 1900544 | bytes 3407872 | tf_op jit(solution)/shard_map/cond/branch_0_fun/add | solution.py:74
  56.2 0.2 multiply_add_fusion.1
  56.5 0.3 multiply_add_fusion
  56.8 0.1 reshape.34
  57.2 0.5 collective-permute-start.7
  57.7 1.9 %collective-permute-start.8 = (f32[4,6,8,128]{3,2,1,0:T(8,128)S(1)}, f32[4,6,8,128]{3,2,1,0:T(8,128)S(1)}, u32[]{:S(2)}, u32[]{:S(2)}) collective-permute-start(f32[4,6,8,128]{3,2,1,0:T(8,128)S(1)} %get-tuple-element.123), channel_id=1, source_target_pairs={{0,8},{8,16},{16,24},{24,32},{32,40},{40,48},{48,56},{56,64},{64,7... | collective-permute-start | bytes 294920 | tf_op jit(solution)/shard_map/ppermute | solution.py:28
  59.6 8.1 %collective-permute-start.9 = (f32[4,6,8,128]{3,2,1,0:T(8,128)S(1)}, f32[4,6,8,128]{3,2,1,0:T(8,128)S(1)}, u32[]{:S(2)}, u32[]{:S(2)}) collective-permute-start(f32[4,6,8,128]{3,2,1,0:T(8,128)S(1)} %get-tuple-element.124), channel_id=1, source_target_pairs={{8,0},{16,8},{24,16},{32,24},{40,32},{48,40},{56,48},{64,56},{72,6... | collective-permute-start | bytes 294920 | tf_op jit(solution)/shard_map/ppermute | solution.py:29
  67.8 0.7 collective-permute-done.8
  68.4 1.5 %collective-permute-done.9 = f32[4,6,8,128]{3,2,1,0:T(8,128)S(1)} collective-permute-done((f32[4,6,8,128]{3,2,1,0:T(8,128)S(1)}, f32[4,6,8,128]{3,2,1,0:T(8,128)S(1)}, u32[]{:S(2)}, u32[]{:S(2)}) %collective-permute-start.9) | collective-permute-done | bytes 98336 | tf_op jit(solution)/shard_map/ppermute | solution.py:29
  70.0 0.2 fusion.38
  70.3 0.9 convolution_bitcast_fusion
  71.2 9.6 %collective-permute-start.11 = (f32[3,4,4096]{2,1,0:T(4,128)S(1)}, f32[3,4,4096]{2,1,0:T(4,128)S(1)}, u32[]{:S(2)}, u32[]{:S(2)}) collective-permute-start(f32[3,4,4096]{2,1,0:T(4,128)S(1)} %get-tuple-element.119), channel_id=1, source_target_pairs={{8,0},{16,8},{24,16},{32,24},{40,32},{48,40},{56,48},{64,56},{72,6... | collective-permute-start | bytes 589832 | tf_op jit(solution)/shard_map/ppermute | solution.py:43
  80.8 1.9 %collective-permute-start.12 = (f32[3,4,4096]{2,1,0:T(4,128)S(1)}, f32[3,4,4096]{2,1,0:T(4,128)S(1)}, u32[]{:S(2)}, u32[]{:S(2)}) collective-permute-start(f32[3,4,4096]{2,1,0:T(4,128)S(1)} %get-tuple-element.120), channel_id=1, source_target_pairs={{248,0},{0,8},{8,16},{16,24},{24,32},{32,40},{40,48},{48,56},{56,6... | collective-permute-start | bytes 589832 | tf_op jit(solution)/shard_map/ppermute | solution.py:43
  82.7 2.8 %collective-permute-done.11 = f32[3,4,4096]{2,1,0:T(4,128)S(1)} collective-permute-done((f32[3,4,4096]{2,1,0:T(4,128)S(1)}, f32[3,4,4096]{2,1,0:T(4,128)S(1)}, u32[]{:S(2)}, u32[]{:S(2)}) %collective-permute-start.11) | collective-permute-done | bytes 196640 | tf_op jit(solution)/shard_map/ppermute | solution.py:43
  85.6 8.9 %collective-permute-done.12 = f32[3,4,4096]{2,1,0:T(4,128)S(1)} collective-permute-done((f32[3,4,4096]{2,1,0:T(4,128)S(1)}, f32[3,4,4096]{2,1,0:T(4,128)S(1)}, u32[]{:S(2)}, u32[]{:S(2)}) %collective-permute-start.12) | collective-permute-done | bytes 196640 | tf_op jit(solution)/shard_map/ppermute | solution.py:43
  94.5 1.3 %collective-permute-start.13 = (f32[3,4,4096]{2,1,0:T(4,128)S(1)}, f32[3,4,4096]{2,1,0:T(4,128)S(1)}, u32[]{:S(2)}, u32[]{:S(2)}) collective-permute-start(f32[3,4,4096]{2,1,0:T(4,128)S(1)} %fusion.40), channel_id=1, source_target_pairs={{0,256},{1,257},{2,258},{3,259},{4,260},{5,261},{6,262},{7,263},{8... | collective-permute-start | bytes 589832 | tf_op jit(solution)/shard_map/ppermute | solution.py:49
  95.8 7.5 %collective-permute-done.13 = f32[3,4,4096]{2,1,0:T(4,128)S(1)} collective-permute-done((f32[3,4,4096]{2,1,0:T(4,128)S(1)}, f32[3,4,4096]{2,1,0:T(4,128)S(1)}, u32[]{:S(2)}, u32[]{:S(2)}) %collective-permute-start.13) | collective-permute-done | bytes 196640 | tf_op jit(solution)/shard_map/ppermute | solution.py:49
  103.4 3.9 %conditional.7 = (f32[4,16,8,128]{3,2,1,0:T(8,128)S(1)}) conditional(s32[]{:T(128)} %convert_element_type.20, (f32[4,28,20,128]{3,2,1,0:T(8,128)S(1)}, f32[3,4,4096]{2,1,0:T(4,128)S(1)}) %tuple.41, () %tuple.42), branch_computations={%region_6.7_spmd, %region_7.8_spmd} | conditional | flops 4505600 | bytes 18874376 | solution.py:158
  103.4 0.1 fusion.76
  103.5 0.1 fusion.77
  103.6 0.1 fusion.78
  103.8 0.1 fusion.79
  103.9 0.1 fusion.80
  104.1 0.1 fusion.81
  104.2 0.1 fusion.82
  104.3 0.1 fusion.83
  104.5 0.1 fusion.72
  104.6 0.1 fusion.73
  104.8 0.1 fusion.74
  104.9 0.1 fusion.75
  105.0 1.4 %fusion.29 = f32[4,16,8,128]{3,2,1,0:T(8,128)S(1)} fusion(f32[4,16,8,1]{3,2,1,0:T(8,128)S(1)} %get-tuple-element.112, f32[4,16,8,127]{3,2,1,0:T(8,128)S(1)} %get-tuple-element.114, f32[4,16,8,127]{3,2,1,0:T(8,128)S(1)} %get-tuple-element.113, f32[4,16,8,1]{3,2,1,0:T(8,128)S(1)} %get-tuple-element.111, f32[4,16,8,2]{3,2,1,0:T(8,128)S(1)} %get-tuple-element.108, ...), kind=kLoop, calls=%fused_computation.80 | loop fusion | flops 1900544 | bytes 3407872 | tf_op jit(solution)/shard_map/cond/branch_0_fun/add | solution.py:74
  106.4 0.2 multiply_add_fusion.3
  106.6 0.3 multiply_add_fusion.2
  107.0 0.1 reshape.37
  107.2 0.8 multiply_bitcast_fusion
  (33 shorter events, 0.8 us)
Async XLA Ops:
  0.0 22.1 %copy-start = (f32[1,4,16,8,128]{4,3,2,1,0:T(8,128)S(1)}, f32[1,4,16,8,128]{4,3,2,1,0:T(8,128)}, u32[]{:S(2)}) copy-start(f32[1,4,16,8,128]{4,3,2,1,0:T(8,128)} %param.11) | copy-start | bytes 786436
  0.0 19.9 %copy-start.2 = (s32[4]{0:T(128)S(1)}, s32[4]{0:T(128)}, u32[]{:S(2)}) copy-start(s32[4]{0:T(128)} %param.12) | copy-start | bytes 52
  0.0 20.0 %copy-start.1 = (f32[4]{0:T(128)S(1)}, f32[4]{0:T(128)}, u32[]{:S(2)}) copy-start(f32[4]{0:T(128)} %param.13) | copy-start | bytes 52
  1.1 21.0 %collective-permute-start = (f32[4,16,6,128]{3,2,1,0:T(8,128)S(1)}, f32[4,16,6,128]{3,2,1,0:T(8,128)S(1)}, u32[]{:S(2)}, u32[]{:S(2)}) collective-permute-start(f32[4,16,6,128]{3,2,1,0:T(8,128)S(1)} %get-tuple-element.129), channel_id=1, source_target_pairs={{0,1},{1,2},{2,3},{3,4},{4,5},{5,6},{6,7},{7,0},{8,9},{9,10},{10,1... | collective-permute-start | bytes 589832 | tf_op jit(solution)/shard_map/ppermute | solution.py:28
  1.2 21.0 %collective-permute-start.3 = (f32[4,16,6,128]{3,2,1,0:T(8,128)S(1)}, f32[4,16,6,128]{3,2,1,0:T(8,128)S(1)}, u32[]{:S(2)}, u32[]{:S(2)}) collective-permute-start(f32[4,16,6,128]{3,2,1,0:T(8,128)S(1)} %get-tuple-element.130), channel_id=1, source_target_pairs={{1,0},{2,1},{3,2},{4,3},{5,4},{6,5},{7,6},{0,7},{9,8},{10,9},{11,1... | collective-permute-start | bytes 589832 | tf_op jit(solution)/shard_map/ppermute | solution.py:29
  5.1 16.3 %collective-permute-start.1 = (f32[4,6,8,128]{3,2,1,0:T(8,128)S(1)}, f32[4,6,8,128]{3,2,1,0:T(8,128)S(1)}, u32[]{:S(2)}, u32[]{:S(2)}) collective-permute-start(f32[4,6,8,128]{3,2,1,0:T(8,128)S(1)} %get-tuple-element.127), channel_id=1, source_target_pairs={{0,8},{8,16},{16,24},{24,32},{32,40},{40,48},{48,56},{56,64},{64,7... | collective-permute-start | bytes 294920 | tf_op jit(solution)/shard_map/ppermute | solution.py:28
  11.2 11.0 %collective-permute-start.2 = (f32[4,6,8,128]{3,2,1,0:T(8,128)S(1)}, f32[4,6,8,128]{3,2,1,0:T(8,128)S(1)}, u32[]{:S(2)}, u32[]{:S(2)}) collective-permute-start(f32[4,6,8,128]{3,2,1,0:T(8,128)S(1)} %get-tuple-element.128), channel_id=1, source_target_pairs={{8,0},{16,8},{24,16},{32,24},{40,32},{48,40},{56,48},{64,56},{72,6... | collective-permute-start | bytes 294920 | tf_op jit(solution)/shard_map/ppermute | solution.py:29
  23.4 11.8 %collective-permute-start.4 = (f32[3,4,4096]{2,1,0:T(4,128)S(1)}, f32[3,4,4096]{2,1,0:T(4,128)S(1)}, u32[]{:S(2)}, u32[]{:S(2)}) collective-permute-start(f32[3,4,4096]{2,1,0:T(4,128)S(1)} %get-tuple-element.121), channel_id=1, source_target_pairs={{8,0},{16,8},{24,16},{32,24},{40,32},{48,40},{56,48},{64,56},{72,6... | collective-permute-start | bytes 589832 | tf_op jit(solution)/shard_map/ppermute | solution.py:43
  32.1 13.4 %collective-permute-start.5 = (f32[3,4,4096]{2,1,0:T(4,128)S(1)}, f32[3,4,4096]{2,1,0:T(4,128)S(1)}, u32[]{:S(2)}, u32[]{:S(2)}) collective-permute-start(f32[3,4,4096]{2,1,0:T(4,128)S(1)} %get-tuple-element.122), channel_id=1, source_target_pairs={{248,0},{0,8},{8,16},{16,24},{24,32},{32,40},{40,48},{48,56},{56,6... | collective-permute-start | bytes 589832 | tf_op jit(solution)/shard_map/ppermute | solution.py:43
  45.6 7.6 %collective-permute-start.6 = (f32[3,4,4096]{2,1,0:T(4,128)S(1)}, f32[3,4,4096]{2,1,0:T(4,128)S(1)}, u32[]{:S(2)}, u32[]{:S(2)}) collective-permute-start(f32[3,4,4096]{2,1,0:T(4,128)S(1)} %fusion.41), channel_id=1, source_target_pairs={{0,256},{1,257},{2,258},{3,259},{4,260},{5,261},{6,262},{7,263},{8... | collective-permute-start | bytes 589832 | tf_op jit(solution)/shard_map/ppermute | solution.py:49
  57.2 12.8 %collective-permute-start.10 = (f32[4,16,6,128]{3,2,1,0:T(8,128)S(1)}, f32[4,16,6,128]{3,2,1,0:T(8,128)S(1)}, u32[]{:S(2)}, u32[]{:S(2)}) collective-permute-start(f32[4,16,6,128]{3,2,1,0:T(8,128)S(1)} %get-tuple-element.126), channel_id=1, source_target_pairs={{1,0},{2,1},{3,2},{4,3},{5,4},{6,5},{7,6},{0,7},{9,8},{10,9},{11,1... | collective-permute-start | bytes 589832 | tf_op jit(solution)/shard_map/ppermute | solution.py:29
  57.2 12.8 %collective-permute-start.7 = (f32[4,16,6,128]{3,2,1,0:T(8,128)S(1)}, f32[4,16,6,128]{3,2,1,0:T(8,128)S(1)}, u32[]{:S(2)}, u32[]{:S(2)}) collective-permute-start(f32[4,16,6,128]{3,2,1,0:T(8,128)S(1)} %get-tuple-element.125), channel_id=1, source_target_pairs={{0,1},{1,2},{2,3},{3,4},{4,5},{5,6},{6,7},{7,0},{8,9},{9,10},{10,1... | collective-permute-start | bytes 589832 | tf_op jit(solution)/shard_map/ppermute | solution.py:28
  57.7 10.7 %collective-permute-start.8 = (f32[4,6,8,128]{3,2,1,0:T(8,128)S(1)}, f32[4,6,8,128]{3,2,1,0:T(8,128)S(1)}, u32[]{:S(2)}, u32[]{:S(2)}) collective-permute-start(f32[4,6,8,128]{3,2,1,0:T(8,128)S(1)} %get-tuple-element.123), channel_id=1, source_target_pairs={{0,8},{8,16},{16,24},{24,32},{32,40},{40,48},{48,56},{56,64},{64,7... | collective-permute-start | bytes 294920 | tf_op jit(solution)/shard_map/ppermute | solution.py:28
  59.6 10.3 %collective-permute-start.9 = (f32[4,6,8,128]{3,2,1,0:T(8,128)S(1)}, f32[4,6,8,128]{3,2,1,0:T(8,128)S(1)}, u32[]{:S(2)}, u32[]{:S(2)}) collective-permute-start(f32[4,6,8,128]{3,2,1,0:T(8,128)S(1)} %get-tuple-element.124), channel_id=1, source_target_pairs={{8,0},{16,8},{24,16},{32,24},{40,32},{48,40},{56,48},{64,56},{72,6... | collective-permute-start | bytes 294920 | tf_op jit(solution)/shard_map/ppermute | solution.py:29
  71.2 14.3 %collective-permute-start.11 = (f32[3,4,4096]{2,1,0:T(4,128)S(1)}, f32[3,4,4096]{2,1,0:T(4,128)S(1)}, u32[]{:S(2)}, u32[]{:S(2)}) collective-permute-start(f32[3,4,4096]{2,1,0:T(4,128)S(1)} %get-tuple-element.119), channel_id=1, source_target_pairs={{8,0},{16,8},{24,16},{32,24},{40,32},{48,40},{56,48},{64,56},{72,6... | collective-permute-start | bytes 589832 | tf_op jit(solution)/shard_map/ppermute | solution.py:43
  80.8 13.6 %collective-permute-start.12 = (f32[3,4,4096]{2,1,0:T(4,128)S(1)}, f32[3,4,4096]{2,1,0:T(4,128)S(1)}, u32[]{:S(2)}, u32[]{:S(2)}) collective-permute-start(f32[3,4,4096]{2,1,0:T(4,128)S(1)} %get-tuple-element.120), channel_id=1, source_target_pairs={{248,0},{0,8},{8,16},{16,24},{24,32},{32,40},{40,48},{48,56},{56,6... | collective-permute-start | bytes 589832 | tf_op jit(solution)/shard_map/ppermute | solution.py:43
  94.5 8.8 %collective-permute-start.13 = (f32[3,4,4096]{2,1,0:T(4,128)S(1)}, f32[3,4,4096]{2,1,0:T(4,128)S(1)}, u32[]{:S(2)}, u32[]{:S(2)}) collective-permute-start(f32[3,4,4096]{2,1,0:T(4,128)S(1)} %fusion.40), channel_id=1, source_target_pairs={{0,256},{1,257},{2,258},{3,259},{4,260},{5,261},{6,262},{7,263},{8... | collective-permute-start | bytes 589832 | tf_op jit(solution)/shard_map/ppermute | solution.py:49
where the time goes:
time: 108 us
  starting transfers between devices  53.1 us (49%)
  waiting for transfers between devices  41.3 us (38%)
  local copies, waits for them, and re-layouts  5.81 us (5%)
  other arithmetic  5.44 us (5%)
  matrix products  1.79 us (2%)
    ppermute x4, waiting for transfers between devices, from_behind(): return lax.ppermute(block, axis, route)  23.2 us
    ppermute x4, starting transfers between devices, from_behind(): return lax.ppermute(block, axis, route)  22.1 us
    ppermute x4, starting transfers between devices, extended_2(): lax.ppermute(first, axis, [(b, a) for a, b in up])  19.9 us
    ppermute x2, waiting for transfers between devices, passed_along(): return lax.ppermute(block, axis, route)  13.8 us
    ppermute x4, starting transfers between devices, extended_2(): lax.ppermute(last, axis, up)  8.52 us
    add x6, other arithmetic, derivative(): total = term if total is None else total + term  3.83 us
    slice x24, local copies, waits for them, and re-layouts, shifted(): return jnp.roll(centre, -offset_j, axis=3)  3.19 us
    ppermute x2, starting transfers between devices, passed_along(): return lax.ppermute(block, axis, route)  2.58 us
  transfers between devices with their start and end apart: 14, of which 10 were waited for; matrix products, arithmetic and copies ran while one was open for 1% of the time, Pallas kernels for 0%

commit v1 on v0

v1 whole, which is shorter than its diff:
```python
import functools

import jax
import jax.numpy as jnp
from jax import lax
from jax.experimental import pallas as pl
from jax.experimental.pallas import tpu as pltpu
from jax.sharding import PartitionSpec as P

drp_weights = (
    0.907646591371,
    -0.337048393268,
    0.133442885327,
    -0.045246480208,
    0.011169294114,
    -0.001456501759,
)
viscosity = 0.05
mean_flow = 0.5
les_time_step = 0.1
ape_time_step = 0.4

MESH = pl.DeviceIdType.MESH
f32 = jnp.float32

BX = 16
BY = 8
NB = 4
BC = BX // NB
NZ = 128
H = 6

(
    LES_XL, LES_XR, LES_YL, LES_YH,
    PRED_XL, PRED_XR, PRED_YL, PRED_YH,
    RAW_HI, RAW_LO, RAW_NEXT,
    RELAY_HI, RELAY_LO,
    TAB_L, TAB_R,
    A1_XL, A1_XR, A1_YLP, A1_YLV, A1_YHP, A1_YHV,
    A2_XL, A2_XR, A2_YLP, A2_YLV, A2_YHP, A2_YHV,
    EDGE_OWN_L, EDGE_OWN_H, EDGE_NEXT_L, EDGE_NEXT_H, EDGE_PREV_L, EDGE_PREV_H,
    EDGE_P_L, EDGE_P_H,
    N_REMOTE,
) = range(36)
L_FLOW, L_YP, L_YV, L_OFF, L_WT, L_OUT, N_LOCAL = range(7)


def sublane():
    return lax.broadcasted_iota(jnp.int32, (BY, NZ), 0)


def cells_of(first, count):
    return pl.ds(first * BY, count * BY)


def row(ref, f, p):
    return jnp.broadcast_to(ref[f, pl.ds(p, 1), :], (BY, NZ))


def around(cells, low, high, f, plane, edge):
    base = pl.multiple_of(plane * BY, BY)
    centre = cells[f, pl.ds(base, BY), :]
    x_m = cells[f, pl.ds(base - BY, BY), :]
    x_p = cells[f, pl.ds(base + BY, BY), :]
    sub = sublane()
    y_m = jnp.where(sub == 0, row(low, f, edge), pltpu.roll(centre, 1, 0))
    y_p = jnp.where(sub == BY - 1, row(high, f, edge), pltpu.roll(centre, BY - 1, 0))
    z_m = pltpu.roll(centre, 1, 1)
    z_p = pltpu.roll(centre, NZ - 1, 1)
    return centre, x_m, x_p, y_m, y_p, z_m, z_p


def lamb_of(near):
    grad = [
        [0.5 * (n[2] - n[1]), 0.5 * (n[4] - n[3]), 0.5 * (n[6] - n[5])] for n in near[:3]
    ]
    u, v, w = near[0][0], near[1][0], near[2][0]
    vort_x = grad[2][1] - grad[1][2]
    vort_y = grad[0][2] - grad[2][0]
    vort_z = grad[1][0] - grad[0][1]
    lamb = (vort_y * w - vort_z * v, vort_z * u - vort_x * w, vort_x * v - vort_y * u)
    return lamb


def spread_of(n):
    return -6.0 * n[0] + n[2] + n[1] + n[4] + n[3] + n[6] + n[5]


def les_tendency(near):
    lamb = lamb_of(near)
    tend = [-lamb[f] + viscosity * spread_of(near[f]) for f in range(3)]
    if len(near) == 4:
        n = near[3]
        carried = (
            near[0][0] * (0.5 * (n[2] - n[1]))
            + near[1][0] * (0.5 * (n[4] - n[3]))
            + near[2][0] * (0.5 * (n[6] - n[5]))
        )
        tend.append(-carried + viscosity * spread_of(n))
    return tend, lamb


def planes(first, last, unroll, body):
    count = last - first
    assert count % unroll == 0

    def step(i, carry):
        for k in range(unroll):
            body(first + i * unroll + k)
        return carry

    lax.fori_loop(0, count // unroll, step, 0)


def kernel(
    gx_size, gy_size,
    flow, flow_planes, offset, weight, out,
    X, XL, XH, EL, EH, XP, PL, PH, QL, QH,
    F, YE, R, RL, RH, SL, SH, V, VL, VH, WL, WH, LB, G, FP, YP, D, TAB, COEF, O,
    off_s, wt_s, send_sem, recv_sem, local_sem,
):
    grp, gx, gy = lax.axis_index("grp"), lax.axis_index("gx"), lax.axis_index("gy")
    right = lax.rem(gx + 1, gx_size)
    left = lax.rem(gx + gx_size - 1, gx_size)
    has_low, has_high = gy > 0, gy < gy_size - 1
    is_les, is_ape = grp == 0, grp == 1

    def copy(kind, src, dst, device):
        return pltpu.make_async_remote_copy(
            src_ref=src,
            dst_ref=dst,
            send_sem=send_sem.at[kind],
            recv_sem=recv_sem.at[kind],
            device_id=device,
            device_id_type=MESH,
        )

    def here(kind, src, dst):
        return pltpu.make_async_copy(src, dst, local_sem.at[kind])

    me_left, me_right = (grp, left, gy), (grp, right, gy)
    me_low, me_high = (grp, gx, gy - 1), (grp, gx, gy + 1)

    les_first = [
        copy(LES_XL, flow.at[:, cells_of(0, 1)], X.at[:, cells_of(BX + 1, 1)], me_left),
        copy(LES_XR, flow.at[:, cells_of(BX - 1, 1)], X.at[:, cells_of(0, 1)], me_right),
    ]
    les_raw = [
        copy(RAW_HI, flow.at[pl.ds(0, 3), cells_of(8, 8)], R.at[:, cells_of(BX + 8, 8)], (1, gx, gy)),
        copy(RAW_LO, flow.at[pl.ds(0, 3), cells_of(0, 8)], R.at[:, cells_of(BX, 8)], (1, gx, gy)),
        copy(
            RAW_NEXT, flow.at[pl.ds(0, 3), cells_of(0, 14)], R.at[:, cells_of(2 * BX, 14)], (1, left, gy)
        ),
    ]
    les_edge_low = copy(LES_YL, EL, XH, me_low)
    les_edge_high = copy(LES_YH, EH, XL, me_high)
    pred_x = [
        copy(PRED_XL, XP.at[:, cells_of(1, 1)], XP.at[:, cells_of(BX + 1, 1)], me_left),
        copy(PRED_XR, XP.at[:, cells_of(BX, 1)], XP.at[:, cells_of(0, 1)], me_right),
    ]
    pred_low = copy(PRED_YL, QL, PH, me_low)
    pred_high = copy(PRED_YH, QH, PL, me_high)

    relay_hi = copy(RELAY_HI, R.at[:, cells_of(BX + 8, 8)], R.at[:, cells_of(8, 8)], me_right)
    relay_lo = copy(RELAY_LO, R.at[:, cells_of(BX + 2, 6)], R.at[:, cells_of(2, 6)], me_right)
    tables = [
        copy(TAB_L, TAB.at[1], TAB.at[2], me_left),
        copy(TAB_R, TAB.at[1], TAB.at[0], me_right),
    ]
    a1_left = copy(A1_XL, flow.at[:, cells_of(0, H)], F.at[:, cells_of(BX + H, H)], me_left)
    a1_right = copy(A1_XR, flow.at[:, cells_of(BX - H, H)], F.at[:, cells_of(0, H)], me_right)
    low_part, own_part, high_part = pl.ds(0, BY), pl.ds(BY, BY), pl.ds(2 * BY, BY)
    a1_low = [
        copy(A1_YLP, flow_planes.at[0], YE.at[0, :, high_part], me_low),
        copy(A1_YLV, flow_planes.at[2], YE.at[1, :, high_part], me_low),
    ]
    a1_high = [
        copy(A1_YHP, flow_planes.at[0], YE.at[0, :, low_part], me_high),
        copy(A1_YHV, flow_planes.at[2], YE.at[1, :, low_part], me_high),
    ]
    own = cells_of(H, BX)
    a2_left = copy(A2_XL, FP.at[:, cells_of(H, H)], FP.at[:, cells_of(BX + H, H)], me_left)
    a2_right = copy(A2_XR, FP.at[:, cells_of(BX, H)], FP.at[:, cells_of(0, H)], me_right)
    a2_low = [
        copy(A2_YLP, YP.at[0, :, own_part], YP.at[0, :, high_part], me_low),
        copy(A2_YLV, YP.at[1, :, own_part], YP.at[1, :, high_part], me_low),
    ]
    a2_high = [
        copy(A2_YHP, YP.at[0, :, own_part], YP.at[0, :, low_part], me_high),
        copy(A2_YHV, YP.at[1, :, own_part], YP.at[1, :, low_part], me_high),
    ]
    third = [pl.ds(0, BX), pl.ds(BX, BX), pl.ds(2 * BX, BX)]

    def edges(kind_low, kind_high, part):
        return (
            copy(kind_low, SL.at[:, third[part]], RH.at[:, third[part]], me_low),
            copy(kind_high, SH.at[:, third[part]], RL.at[:, third[part]], me_high),
        )

    edge_own = edges(EDGE_OWN_L, EDGE_OWN_H, 1)
    edge_next = edges(EDGE_NEXT_L, EDGE_NEXT_H, 2)
    edge_prev = edges(EDGE_PREV_L, EDGE_PREV_H, 0)
    edge_pred = (copy(EDGE_P_L, WL, VH, me_low), copy(EDGE_P_H, WH, VL, me_high))

    @pl.when(is_les)
    def _():
        here(L_FLOW, flow, X.at[:, cells_of(1, BX)]).start()

    @pl.when(is_ape)
    def _():
        here(L_FLOW, flow, F.at[:, own]).start()
        here(L_YP, flow_planes.at[0], YE.at[0, :, own_part]).start()
        here(L_YV, flow_planes.at[2], YE.at[1, :, own_part]).start()
        here(L_OFF, offset, off_s).start()
        here(L_WT, weight, wt_s).start()

    barrier = pltpu.get_barrier_semaphore()

    def greet(device):
        pl.semaphore_signal(barrier, inc=1, device_id=device, device_id_type=MESH)

    greet(me_left)
    greet(me_right)
    greet((1 - grp, gx, gy))

    @pl.when(is_les)
    def _():
        greet((1, left, gy))

    @pl.when(is_ape)
    def _():
        greet((0, right, gy))

    @pl.when(has_low)
    def _():
        greet(me_low)

    @pl.when(has_high)
    def _():
        greet(me_high)

    zeros_edge = jnp.zeros((48, NZ), f32)

    @pl.when(jnp.logical_not(has_low))
    def _():
        for f in range(4):
            XL[f] = zeros_edge[:BX]
            PL[f] = zeros_edge[:BX]
        for f in range(3):
            RL[f] = zeros_edge
            VL[f] = zeros_edge
        for f in range(2):
            YE[f, :, pl.ds(0, BY)] = jnp.zeros((BX, BY, NZ), f32)
            YP[f, :, pl.ds(0, BY)] = jnp.zeros((BX, BY, NZ), f32)

    @pl.when(jnp.logical_not(has_high))
    def _():
        for f in range(4):
            XH[f] = zeros_edge[:BX]
            PH[f] = zeros_edge[:BX]
        for f in range(3):
            RH[f] = zeros_edge
            VH[f] = zeros_edge
        for f in range(2):
            YE[f, :, pl.ds(2 * BY, BY)] = jnp.zeros((BX, BY, NZ), f32)
            YP[f, :, pl.ds(2 * BY, BY)] = jnp.zeros((BX, BY, NZ), f32)

    y_neighbours = jnp.where(has_low, 1, 0) + jnp.where(has_high, 1, 0)

    def exchange(low, high, what):
        @pl.when(has_low)
        def _():
            getattr(low, what)()

        @pl.when(has_high)
        def _():
            getattr(high, what)()

    def pack(cells, first, count, low, high, at, fields):
        for f in range(fields):
            low[f, pl.ds(at, count), :] = cells[f, pl.ds(first * BY, count, stride=BY), :]
            high[f, pl.ds(at, count), :] = cells[
                f, pl.ds(first * BY + BY - 1, count, stride=BY), :
            ]

    @pl.when(is_les)
    def les():
        pl.semaphore_wait(barrier, 4 + y_neighbours)
        for c in les_first + les_raw:
            c.start()
        cells, ahead, final = X, XP, O
        here(L_FLOW, flow, X.at[:, cells_of(1, BX)]).wait()
        pack(cells, 1, BX, EL, EH, 0, 4)
        exchange(les_edge_low, les_edge_high, "start")
        for c in les_first:
            c.wait_recv()
        exchange(les_edge_high, les_edge_low, "wait_recv")

        def predict(x):
            near = [around(cells, XL, XH, f, x + 1, x) for f in range(4)]
            tend, _ = les_tendency(near)
            for f in range(4):
                ahead[f, pl.ds(pl.multiple_of((x + 1) * BY, BY), BY), :] = (
                    near[f][0] + les_time_step * tend[f]
                )

        planes(0, BX, 2, predict)
        for c in pred_x:
            c.start()
        pack(ahead, 1, BX, QL, QH, 0, 4)
        exchange(pred_low, pred_high, "start")
        for c in pred_x:
            c.wait_recv()
        exchange(pred_high, pred_low, "wait_recv")

        def correct(x):
            near = [around(ahead, PL, PH, f, x + 1, x) for f in range(4)]
            tend, _ = les_tendency(near)
            for f in range(4):
                before = cells[f, pl.ds(pl.multiple_of((x + 1) * BY, BY), BY), :]
                final[f, pl.ds(pl.multiple_of(x * BY, BY), BY), :] = 0.5 * (
                    before + near[f][0] + les_time_step * tend[f]
                )

        planes(0, BX, 2, correct)
        here(L_OUT, O, out).start()
        for c in les_first + les_raw + pred_x:
            c.wait_send()
        exchange(les_edge_low, les_edge_high, "wait_send")
        exchange(pred_low, pred_high, "wait_send")
        here(L_OUT, O, out).wait()

    @pl.when(is_ape)
    def ape():
        raw, state, ahead, moved, rate, state_p, dep, final = R, F, V, LB, G, FP, D, O

        here(L_OFF, offset, off_s).wait()
        here(L_WT, weight, wt_s).wait()
        sub = sublane()
        table = jnp.zeros((BY, NZ), f32)
        for b in range(NB):
            table = jnp.where(sub == b, off_s[b].astype(f32), table)
            table = jnp.where(sub == NB + b, wt_s[b], table)
        TAB[1] = table

        pl.semaphore_wait(barrier, 4 + y_neighbours)
        a1_left.start()
        for low, high in zip(a1_low, a1_high):
            exchange(low, high, "start")
        for c in tables:
            c.start()

        les_raw[0].wait_recv()
        relay_hi.start()
        les_raw[1].wait_recv()
        relay_lo.start()
        a1_right.start()
        pack(raw, BX, BX, SL, SH, BX, 3)
        exchange(*edge_own, "start")

        here(L_FLOW, flow, F.at[:, own]).wait()
        here(L_YP, flow_planes.at[0], YE.at[0, :, own_part]).wait()
        here(L_YV, flow_planes.at[2], YE.at[1, :, own_part]).wait()

        def thirteen(plus, minus):
            total = None
            for j, c in enumerate(drp_weights, start=1):
                term = c * (plus(j) - minus(j))
                total = term if total is None else total + term
            return total

        def rate_yz(cells, walls):
            def body(x):
                at = pl.multiple_of((x + H) * BY, BY)
                to = pl.ds(pl.multiple_of(x * BY, BY), BY)
                p, w = cells[0, pl.ds(at, BY), :], cells[3, pl.ds(at, BY), :]
                dz = [
                    thirteen(lambda j: pltpu.roll(q, NZ - j, 1), lambda j: pltpu.roll(q, j, 1))
                    for q in (p, w)
                ]
                dy = [
                    thirteen(
                        lambda j: walls[f, x, pl.ds(BY + j, BY), :],
                        lambda j: walls[f, x, pl.ds(BY - j, BY), :],
                    )
                    for f in range(2)
                ]
                rate[0, to, :] = -(dy[1] + dz[1])
                rate[2, to, :] = -dy[0]
                rate[3, to, :] = -dz[0]

            planes(0, BX, 2, body)

        def rate_x(cells, x):
            at = (x + H) * BY

            def along(f):
                return thirteen(
                    lambda j: cells[f, pl.ds(pl.multiple_of(at + j * BY, BY), BY), :],
                    lambda j: cells[f, pl.ds(pl.multiple_of(at - j * BY, BY), BY), :],
                )

            to = pl.ds(pl.multiple_of(x * BY, BY), BY)
            dx = [along(f) for f in range(4)]
            return (
                rate[0, to, :] - mean_flow * dx[0] - dx[1],
                -mean_flow * dx[1] - dx[0],
                rate[2, to, :] - mean_flow * dx[2],
                rate[3, to, :] - mean_flow * dx[3],
            )

        for low, high in zip(a1_low, a1_high):
            exchange(high, low, "wait_recv")
        rate_yz(state, YE)

        les_raw[2].wait_recv()
        pack(raw, 2 * BX, BX, SL, SH, 2 * BX, 3)
        exchange(*edge_next, "start")

        for c in tables:
            c.wait_recv()
        pairs = []
        for d in range(NB):
            for part, shift in enumerate((NB, 0, -NB)):
                for b in range(NB):
                    near_block, far_block = 1 - NB, NB
                    lowest = b + (near_block if b < NB - 1 else 0)
                    highest = b + (far_block if b > 0 else 0)
                    if lowest <= d + shift <= highest:
                        pairs.append((d, part, b, d + shift))
        for k, (d, part, b, aim) in enumerate(pairs):
            target = row(TAB, part, b) + float(b)
            share = row(TAB, part, NB + b)
            COEF[k] = jnp.where(target == float(aim), share, 0.0) + jnp.where(
                target + 1.0 == float(aim), 1.0 - share, 0.0
            )

        def first_lamb(p):
            near = [around(raw, RL, RH, f, p, p) for f in range(3)]
            tend, lamb = les_tendency(near)
            to = pl.ds(pl.multiple_of(p * BY, BY), BY)
            for f in range(3):
                ahead[f, to, :] = near[f][0] + les_time_step * tend[f]
                moved[f, to, :] = lamb[f]

        def second_lamb(p):
            near = [around(ahead, VL, VH, f, p, p) for f in range(3)]
            lamb = lamb_of(near)
            to = pl.ds(pl.multiple_of(p * BY, BY), BY)
            for f in range(3):
                moved[f, to, :] = lamb[f]

        def deposit():
            for d in range(NB):
                terms = [(k, q[1] * BX + q[2] * BC) for k, q in enumerate(pairs) if q[0] == d]

                def body(r, carry):
                    for f in range(3):
                        total = None
                        for k, first in terms:
                            at = pl.multiple_of((first + r) * BY, BY)
                            term = COEF[k] * moved[f, pl.ds(at, BY), :]
                            total = term if total is None else total + term
                        to = pl.multiple_of((d * BC + r) * BY, BY)
                        dep[f, pl.ds(to, BY), :] = total
                    return carry

                lax.fori_loop(0, BC, body, 0)

        exchange(edge_own[1], edge_own[0], "wait_recv")
        exchange(edge_next[1], edge_next[0], "wait_recv")
        planes(BX + 1, BX + 29, 2, first_lamb)

        relay_hi.wait_recv()
        relay_lo.wait_recv()
        pack(raw, 0, BX, SL, SH, 0, 3)
        exchange(*edge_prev, "start")
        exchange(edge_prev[1], edge_prev[0], "wait_recv")
        planes(3, BX + 1, 2, first_lamb)
        pack(ahead, 0, 3 * BX, WL, WH, 0, 3)
        exchange(*edge_pred, "start")
        deposit()

        a1_left.wait_recv()
        a1_right.wait_recv()

        def predict(x):
            tend = rate_x(state, x)
            at = pl.ds(pl.multiple_of((x + H) * BY, BY), BY)
            to = pl.ds(pl.multiple_of(x * BY, BY), BY)
            for f in range(4):
                t = tend[f] - dep[f - 1, to, :] if f else tend[f]
                predicted = state[f, at, :] + ape_time_step * t
                state_p[f, at, :] = predicted
                if f in (0, 2):
                    YP[f // 2, x, own_part, :] = predicted

        planes(0, BX, 2, predict)
        a2_left.start()
        a2_right.start()
        for low, high in zip(a2_low, a2_high):
            exchange(low, high, "start")

        exchange(edge_pred[1], edge_pred[0], "wait_recv")
        planes(4, 44, 2, second_lamb)
        deposit()
        for low, high in zip(a2_low, a2_high):
            exchange(high, low, "wait_recv")
        rate_yz(state_p, YP)
        a2_left.wait_recv()
        a2_right.wait_recv()

        def correct(x):
            tend = rate_x(state_p, x)
            at = pl.ds(pl.multiple_of((x + H) * BY, BY), BY)
            to = pl.ds(pl.multiple_of(x * BY, BY), BY)
            for f in range(4):
                t = tend[f] - dep[f - 1, to, :] if f else tend[f]
                final[f, to, :] = 0.5 * (
                    state[f, at, :] + state_p[f, at, :] + ape_time_step * t
                )

        planes(0, BX, 2, correct)
        here(L_OUT, O, out).start()
        for c in tables + [relay_hi, relay_lo, a1_left, a1_right, a2_left, a2_right]:
            c.wait_send()
        for pair in (edge_own, edge_next, edge_prev, edge_pred):
            exchange(*pair, "wait_send")
        for lows, highs in ((a1_low, a1_high), (a2_low, a2_high)):
            for low, high in zip(lows, highs):
                exchange(low, high, "wait_send")
        here(L_OUT, O, out).wait()


def on_device(flow_state, block_offset, block_weight):
    gx_size, gy_size = lax.axis_size("gx"), lax.axis_size("gy")

    def vmem(*shape):
        return pltpu.VMEM(shape, f32)

    def planes_of(fields, count):
        return vmem(fields, count * BY, NZ)

    scratch = [
        planes_of(4, BX + 2),
        *[vmem(4, BX, NZ)] * 4,
        planes_of(4, BX + 2),
        *[vmem(4, BX, NZ)] * 4,
        planes_of(4, BX + 2 * H),
        vmem(2, BX, 3 * BY, NZ),
        planes_of(3, 3 * BX),
        *[vmem(3, 3 * BX, NZ)] * 4,
        planes_of(3, 3 * BX),
        *[vmem(3, 3 * BX, NZ)] * 4,
        planes_of(3, 3 * BX),
        planes_of(4, BX),
        planes_of(4, BX + 2 * H),
        vmem(2, BX, 3 * BY, NZ),
        planes_of(3, BX),
        vmem(3, BY, NZ),
        vmem(25, BY, NZ),
        planes_of(4, BX),
        pltpu.SMEM((NB,), jnp.int32),
        pltpu.SMEM((NB,), f32),
        pltpu.SemaphoreType.DMA((N_REMOTE,)),
        pltpu.SemaphoreType.DMA((N_REMOTE,)),
        pltpu.SemaphoreType.DMA((N_LOCAL,)),
    ]
    anywhere = pl.BlockSpec(memory_space=pl.ANY)
    advanced = pl.pallas_call(
        functools.partial(kernel, gx_size, gy_size),
        out_shape=jax.ShapeDtypeStruct((4, BX * BY, NZ), f32),
        in_specs=[anywhere] * 4,
        out_specs=anywhere,
        scratch_shapes=scratch,
        compiler_params=pltpu.CompilerParams(collective_id=0, has_side_effects=True),
        name="heun",
    )(flow_state.reshape(4, BX * BY, NZ), flow_state[0], block_offset, block_weight)
    return advanced.reshape(flow_state.shape)


def solution(mesh):
    placed = (P("grp", None, "gx", "gy", None), P("gx"), P("gx"))
    return jax.shard_map(
        on_device,
        mesh=mesh,
        in_specs=placed,
        out_specs=P("grp", None, "gx", "gy", None),
        check_vma=False,
    )
```

time: 108 us -> 40.4 us (0.37)
  the two profiles are of different devices: /device:TPU:64 before, /device:TPU:66 now
where the time goes in v1:
time: 40.4 us; the launch traced here: 40.3 us
  Pallas kernels  38.6 us (96%)
  local copies, waits for them, and re-layouts  1.67 us (4%)
    pallas_call x1, Pallas kernels, on_device(): pl.pallas_call(functools.partial(kernel, gx_size, gy_size), out_shape=jax...  38.6 us
    unnamed x1, local copies, waits for them, and re-layouts  1.67 us

profile of v1, /device:TPU:66, one launch (start us, length us, event | category | flops | bytes accessed | tf_op | source)
XLA Modules:
  0.0 40.3 jit_solution(18120950359076322482)
XLA Ops:
  0.0 38.6 %heun.1 = f32[4,128,128]{2,1,0:T(8,128)} custom-call(f32[4,128,128]{2,1,0:T(8,128)} %bitcast.3, f32[4,16,8,128]{3,2,1,0:T(8,128)} %bitcast.4, s32[4]{0:T(128)} %offset.1, f32[4]{0:T(128)} %weight.1), custom_call_target="tpu_custom_call" | custom-call | tf_op jit(solution)/shard_map/heun/pallas_call | solution.py:570
  38.6 1.7 %copy.5 = f32[1,4,16,8,128]{4,3,2,1,0:T(8,128)} copy(f32[1,4,16,8,128]{4,3,2,1,0:T(8,128)} %bitcast.5) | data formatting | bytes 524288

commit v2 on v1

--- a/solution.py
+++ b/solution.py
@@ -33,15 +33,15 @@
 (
     LES_XL, LES_XR, LES_YL, LES_YH,
     PRED_XL, PRED_XR, PRED_YL, PRED_YH,
-    RAW_HI, RAW_LO, RAW_NEXT,
-    RELAY_HI, RELAY_LO,
+    RAW_0, RAW_1, RAW_2, RAW_3, RAW_NEXT,
+    RELAY_0, RELAY_1, RELAY_2, RELAY_3,
     TAB_L, TAB_R,
     A1_XL, A1_XR, A1_YLP, A1_YLV, A1_YHP, A1_YHV,
-    A2_XL, A2_XR, A2_YLP, A2_YLV, A2_YHP, A2_YHV,
+    A2_XL, A2_XR, A2_XLP, A2_XRP, A2_YLP, A2_YLV, A2_YHP, A2_YHV,
     EDGE_OWN_L, EDGE_OWN_H, EDGE_NEXT_L, EDGE_NEXT_H, EDGE_PREV_L, EDGE_PREV_H,
-    EDGE_P_L, EDGE_P_H,
+    EDGE_P_L, EDGE_P_H, LATE_P_L, LATE_P_H,
     N_REMOTE,
-) = range(36)
+) = range(44)
 L_FLOW, L_YP, L_YV, L_OFF, L_WT, L_OUT, N_LOCAL = range(7)
 
 
@@ -116,7 +116,7 @@
     gx_size, gy_size,
     flow, flow_planes, offset, weight, out,
     X, XL, XH, EL, EH, XP, PL, PH, QL, QH,
-    F, YE, R, RL, RH, SL, SH, V, VL, VH, WL, WH, LB, G, FP, YP, D, TAB, COEF, O,
+    F, YE, R, RL, RH, V, VL, VH, WL, WH, LB, LC, G, FP, YP, D, E, TAB, COEF,
     off_s, wt_s, send_sem, recv_sem, local_sem,
 ):
     grp, gx, gy = lax.axis_index("grp"), lax.axis_index("gx"), lax.axis_index("gy")
@@ -145,13 +145,20 @@
         copy(LES_XL, flow.at[:, cells_of(0, 1)], X.at[:, cells_of(BX + 1, 1)], me_left),
         copy(LES_XR, flow.at[:, cells_of(BX - 1, 1)], X.at[:, cells_of(0, 1)], me_right),
     ]
+    pieces = [(12, 4), (8, 4), (4, 4), (0, 4)]
+    velocity = pl.ds(0, 3)
     les_raw = [
-        copy(RAW_HI, flow.at[pl.ds(0, 3), cells_of(8, 8)], R.at[:, cells_of(BX + 8, 8)], (1, gx, gy)),
-        copy(RAW_LO, flow.at[pl.ds(0, 3), cells_of(0, 8)], R.at[:, cells_of(BX, 8)], (1, gx, gy)),
         copy(
-            RAW_NEXT, flow.at[pl.ds(0, 3), cells_of(0, 14)], R.at[:, cells_of(2 * BX, 14)], (1, left, gy)
-        ),
-    ]
+            RAW_0 + k,
+            flow.at[velocity, cells_of(first, count)],
+            R.at[:, cells_of(BX + first, count)],
+            (1, gx, gy),
+        )
+        for k, (first, count) in enumerate(pieces)
+    ]
+    les_next = copy(
+        RAW_NEXT, flow.at[velocity, cells_of(0, 14)], R.at[:, cells_of(2 * BX, 14)], (1, left, gy)
+    )
     les_edge_low = copy(LES_YL, EL, XH, me_low)
     les_edge_high = copy(LES_YH, EH, XL, me_high)
     pred_x = [
@@ -161,8 +168,18 @@
     pred_low = copy(PRED_YL, QL, PH, me_low)
     pred_high = copy(PRED_YH, QH, PL, me_high)
 
-    relay_hi = copy(RELAY_HI, R.at[:, cells_of(BX + 8, 8)], R.at[:, cells_of(8, 8)], me_right)
-    relay_lo = copy(RELAY_LO, R.at[:, cells_of(BX + 2, 6)], R.at[:, cells_of(2, 6)], me_right)
+    relays = []
+    for k, (first, count) in enumerate(pieces):
+        start = max(first, 2)
+        count = first + count - start
+        relays.append(
+            copy(
+                RELAY_0 + k,
+                R.at[:, cells_of(BX + start, count)],
+                R.at[:, cells_of(start, count)],
+                me_right,
+            )
+        )
     tables = [
         copy(TAB_L, TAB.at[1], TAB.at[2], me_left),
         copy(TAB_R, TAB.at[1], TAB.at[0], me_right),
@@ -179,8 +196,11 @@
         copy(A1_YHV, flow_planes.at[2], YE.at[1, :, low_part], me_high),
     ]
     own = cells_of(H, BX)
-    a2_left = copy(A2_XL, FP.at[:, cells_of(H, H)], FP.at[:, cells_of(BX + H, H)], me_left)
-    a2_right = copy(A2_XR, FP.at[:, cells_of(BX, H)], FP.at[:, cells_of(0, H)], me_right)
+    flows = pl.ds(1, 3)
+    a2_left = copy(A2_XL, FP.at[flows, cells_of(H, H)], FP.at[flows, cells_of(BX + H, H)], me_left)
+    a2_right = copy(A2_XR, FP.at[flows, cells_of(BX, H)], FP.at[flows, cells_of(0, H)], me_right)
+    a2_left_p = copy(A2_XLP, FP.at[0, cells_of(H, H)], FP.at[0, cells_of(BX + H, H)], me_left)
+    a2_right_p = copy(A2_XRP, FP.at[0, cells_of(BX, H)], FP.at[0, cells_of(0, H)], me_right)
     a2_low = [
         copy(A2_YLP, YP.at[0, :, own_part], YP.at[0, :, high_part], me_low),
         copy(A2_YLV, YP.at[1, :, own_part], YP.at[1, :, high_part], me_low),
@@ -191,16 +211,27 @@
     ]
     third = [pl.ds(0, BX), pl.ds(BX, BX), pl.ds(2 * BX, BX)]
 
-    def edges(kind_low, kind_high, part):
-        return (
-            copy(kind_low, SL.at[:, third[part]], RH.at[:, third[part]], me_low),
-            copy(kind_high, SH.at[:, third[part]], RL.at[:, third[part]], me_high),
-        )
-
-    edge_own = edges(EDGE_OWN_L, EDGE_OWN_H, 1)
-    edge_next = edges(EDGE_NEXT_L, EDGE_NEXT_H, 2)
-    edge_prev = edges(EDGE_PREV_L, EDGE_PREV_H, 0)
-    edge_pred = (copy(EDGE_P_L, WL, VH, me_low), copy(EDGE_P_H, WH, VL, me_high))
+    edge_own = (
+        copy(EDGE_OWN_L, EL.at[velocity], RH.at[:, third[1]], (1, gx, gy - 1)),
+        copy(EDGE_OWN_H, EH.at[velocity], RL.at[:, third[1]], (1, gx, gy + 1)),
+    )
+    edge_next = (
+        copy(EDGE_NEXT_L, EL.at[velocity], RH.at[:, third[2]], (1, left, gy - 1)),
+        copy(EDGE_NEXT_H, EH.at[velocity], RL.at[:, third[2]], (1, left, gy + 1)),
+    )
+    edge_prev = (
+        copy(EDGE_PREV_L, RL.at[:, third[1]], RL.at[:, third[0]], me_right),
+        copy(EDGE_PREV_H, RH.at[:, third[1]], RH.at[:, third[0]], me_right),
+    )
+    soon, late = pl.ds(BX, 2 * BX), pl.ds(0, BX)
+    edge_pred = (
+        copy(EDGE_P_L, WL.at[:, soon], VH.at[:, soon], me_low),
+        copy(EDGE_P_H, WH.at[:, soon], VL.at[:, soon], me_high),
+    )
+    late_pred = (
+        copy(LATE_P_L, WL.at[:, late], VH.at[:, late], me_low),
+        copy(LATE_P_H, WH.at[:, late], VL.at[:, late], me_high),
+    )
 
     @pl.when(is_les)
     def _():
@@ -227,9 +258,29 @@
     def _():
         greet((1, left, gy))
 
+        @pl.when(has_low)
+        def _():
+            greet((1, gx, gy - 1))
+            greet((1, left, gy - 1))
+
+        @pl.when(has_high)
+        def _():
+            greet((1, gx, gy + 1))
+            greet((1, left, gy + 1))
+
     @pl.when(is_ape)
     def _():
         greet((0, right, gy))
+
+        @pl.when(has_low)
+        def _():
+            greet((0, gx, gy - 1))
+            greet((0, right, gy - 1))
+
+        @pl.when(has_high)
+        def _():
+            greet((0, gx, gy + 1))
+            greet((0, right, gy + 1))
 
     @pl.when(has_low)
     def _():
@@ -285,12 +336,14 @@
 
     @pl.when(is_les)
     def les():
-        pl.semaphore_wait(barrier, 4 + y_neighbours)
-        for c in les_first + les_raw:
-            c.start()
-        cells, ahead, final = X, XP, O
+        cells, ahead, final = X, XP, out
         here(L_FLOW, flow, X.at[:, cells_of(1, BX)]).wait()
         pack(cells, 1, BX, EL, EH, 0, 4)
+        pl.semaphore_wait(barrier, 4 + 3 * y_neighbours)
+        exchange(*edge_own, "start")
+        exchange(*edge_next, "start")
+        for c in les_raw + [les_next] + les_first:
+            c.start()
         exchange(les_edge_low, les_edge_high, "start")
         for c in les_first:
             c.wait_recv()
@@ -323,16 +376,16 @@
                 )
 
         planes(0, BX, 2, correct)
-        here(L_OUT, O, out).start()
-        for c in les_first + les_raw + pred_x:
+        for c in les_raw + [les_next] + les_first + pred_x:
             c.wait_send()
         exchange(les_edge_low, les_edge_high, "wait_send")
         exchange(pred_low, pred_high, "wait_send")
-        here(L_OUT, O, out).wait()
+        exchange(*edge_own, "wait_send")
+        exchange(*edge_next, "wait_send")
 
     @pl.when(is_ape)
     def ape():
-        raw, state, ahead, moved, rate, state_p, dep, final = R, F, V, LB, G, FP, D, O
+        raw, state, ahead, rate, state_p, final = R, F, V, G, FP, out
 
         here(L_OFF, offset, off_s).wait()
         here(L_WT, weight, wt_s).wait()
@@ -343,24 +396,13 @@
             table = jnp.where(sub == NB + b, wt_s[b], table)
         TAB[1] = table
 
-        pl.semaphore_wait(barrier, 4 + y_neighbours)
+        pl.semaphore_wait(barrier, 4 + 3 * y_neighbours)
+        for c in tables:
+            c.start()
+        a1_right.start()
         a1_left.start()
         for low, high in zip(a1_low, a1_high):
             exchange(low, high, "start")
-        for c in tables:
-            c.start()
-
-        les_raw[0].wait_recv()
-        relay_hi.start()
-        les_raw[1].wait_recv()
-        relay_lo.start()
-        a1_right.start()
-        pack(raw, BX, BX, SL, SH, BX, 3)
-        exchange(*edge_own, "start")
-
-        here(L_FLOW, flow, F.at[:, own]).wait()
-        here(L_YP, flow_planes.at[0], YE.at[0, :, own_part]).wait()
-        here(L_YV, flow_planes.at[2], YE.at[1, :, own_part]).wait()
 
         def thirteen(plus, minus):
             total = None
@@ -369,7 +411,7 @@
                 total = term if total is None else total + term
             return total
 
-        def rate_yz(cells, walls):
+        def rate_z(cells):
             def body(x):
                 at = pl.multiple_of((x + H) * BY, BY)
                 to = pl.ds(pl.multiple_of(x * BY, BY), BY)
@@ -378,6 +420,14 @@
                     thirteen(lambda j: pltpu.roll(q, NZ - j, 1), lambda j: pltpu.roll(q, j, 1))
                     for q in (p, w)
                 ]
+                rate[0, to, :] = -dz[1]
+                rate[3, to, :] = -dz[0]
+
+            planes(0, BX, 2, body)
+
+        def rate_y(walls):
+            def body(x):
+                to = pl.ds(pl.multiple_of(x * BY, BY), BY)
                 dy = [
                     thirteen(
                         lambda j: walls[f, x, pl.ds(BY + j, BY), :],
@@ -385,9 +435,8 @@
                     )
                     for f in range(2)
                 ]
-                rate[0, to, :] = -(dy[1] + dz[1])
+                rate[0, to, :] = rate[0, to, :] - dy[1]
                 rate[2, to, :] = -dy[0]
-                rate[3, to, :] = -dz[0]
 
             planes(0, BX, 2, body)
 
@@ -409,16 +458,9 @@
                 rate[3, to, :] - mean_flow * dx[3],
             )
 
-        for low, high in zip(a1_low, a1_high):
-            exchange(high, low, "wait_recv")
-        rate_yz(state, YE)
-
-        les_raw[2].wait_recv()
-        pack(raw, 2 * BX, BX, SL, SH, 2 * BX, 3)
-        exchange(*edge_next, "start")
-
-        for c in tables:
-            c.wait_recv()
+        here(L_FLOW, flow, F.at[:, own]).wait()
+        rate_z(state)
+
         pairs = []
         for d in range(NB):
             for part, shift in enumerate((NB, 0, -NB)):
@@ -428,12 +470,6 @@
                     highest = b + (far_block if b > 0 else 0)
                     if lowest <= d + shift <= highest:
                         pairs.append((d, part, b, d + shift))
-        for k, (d, part, b, aim) in enumerate(pairs):
-            target = row(TAB, part, b) + float(b)
-            share = row(TAB, part, NB + b)
-            COEF[k] = jnp.where(target == float(aim), share, 0.0) + jnp.where(
-                target + 1.0 == float(aim), 1.0 - share, 0.0
-            )
 
         def first_lamb(p):
             near = [around(raw, RL, RH, f, p, p) for f in range(3)]
@@ -441,18 +477,22 @@
             to = pl.ds(pl.multiple_of(p * BY, BY), BY)
             for f in range(3):
                 ahead[f, to, :] = near[f][0] + les_time_step * tend[f]
-                moved[f, to, :] = lamb[f]
+                LB[f, to, :] = lamb[f]
 
         def second_lamb(p):
-            near = [around(ahead, VL, VH, f, p, p) for f in range(3)]
+            near = [around(ahead, VL, VH, f, p, p - 1) for f in range(3)]
             lamb = lamb_of(near)
             to = pl.ds(pl.multiple_of(p * BY, BY), BY)
             for f in range(3):
-                moved[f, to, :] = lamb[f]
-
-        def deposit():
+                LC[f, to, :] = lamb[f]
+
+        def deposit(moved, is_late, add):
             for d in range(NB):
-                terms = [(k, q[1] * BX + q[2] * BC) for k, q in enumerate(pairs) if q[0] == d]
+                terms = [
+                    (k, part * BX + b * BC)
+                    for k, (to, part, b, _) in enumerate(pairs)
+                    if to == d and is_late == (part * NB + b <= NB)
+                ]
 
                 def body(r, carry):
                     for f in range(3):
@@ -461,25 +501,55 @@
                             at = pl.multiple_of((first + r) * BY, BY)
                             term = COEF[k] * moved[f, pl.ds(at, BY), :]
                             total = term if total is None else total + term
-                        to = pl.multiple_of((d * BC + r) * BY, BY)
-                        dep[f, pl.ds(to, BY), :] = total
+                        add(f, d * BC + r, total)
                     return carry
 
                 lax.fori_loop(0, BC, body, 0)
 
+        def keep_in(ref):
+            def add(f, x, total):
+                ref[f, pl.ds(pl.multiple_of(x * BY, BY), BY), :] = total
+
+            return add
+
         exchange(edge_own[1], edge_own[0], "wait_recv")
+        exchange(*edge_prev, "start")
+        for k in range(2):
+            les_raw[k].wait_recv()
+            relays[k].start()
+        planes(BX + 9, BX + 15, 2, first_lamb)
+        les_raw[2].wait_recv()
+        relays[2].start()
+        planes(BX + 5, BX + 9, 2, first_lamb)
+        les_raw[3].wait_recv()
+        relays[3].start()
+        planes(BX + 1, BX + 5, 2, first_lamb)
+
         exchange(edge_next[1], edge_next[0], "wait_recv")
-        planes(BX + 1, BX + 29, 2, first_lamb)
-
-        relay_hi.wait_recv()
-        relay_lo.wait_recv()
-        pack(raw, 0, BX, SL, SH, 0, 3)
-        exchange(*edge_prev, "start")
-        exchange(edge_prev[1], edge_prev[0], "wait_recv")
-        planes(3, BX + 1, 2, first_lamb)
-        pack(ahead, 0, 3 * BX, WL, WH, 0, 3)
+        les_next.wait_recv()
+        planes(2 * BX - 1, 2 * BX + 13, 2, first_lamb)
+        pack(ahead, BX + 1, 28, WL, WH, BX, 3)
         exchange(*edge_pred, "start")
-        deposit()
+        for c in tables:
+            c.wait_recv()
+        for k, (d, part, b, aim) in enumerate(pairs):
+            target = row(TAB, part, b) + float(b)
+            share = row(TAB, part, NB + b)
+            COEF[k] = jnp.where(target == float(aim), share, 0.0) + jnp.where(
+                target + 1.0 == float(aim), 1.0 - share, 0.0
+            )
+        deposit(LB, False, keep_in(D))
+
+        here(L_YP, flow_planes.at[0], YE.at[0, :, own_part]).wait()
+        here(L_YV, flow_planes.at[2], YE.at[1, :, own_part]).wait()
+        for low, high in zip(a1_low, a1_high):
+            exchange(high, low, "wait_recv")
+        rate_y(YE)
+
+        exchange(*edge_prev, "wait_recv")
+        for k, (first, last) in enumerate(((13, 17), (9, 13), (5, 9), (3, 5))):
+            relays[k].wait_recv()
+            planes(first, last, 2, first_lamb)
 
         a1_left.wait_recv()
         a1_right.wait_recv()
@@ -489,47 +559,69 @@
             at = pl.ds(pl.multiple_of((x + H) * BY, BY), BY)
             to = pl.ds(pl.multiple_of(x * BY, BY), BY)
             for f in range(4):
-                t = tend[f] - dep[f - 1, to, :] if f else tend[f]
+                t = tend[f] - D[f - 1, to, :] if f else tend[f]
                 predicted = state[f, at, :] + ape_time_step * t
                 state_p[f, at, :] = predicted
-                if f in (0, 2):
-                    YP[f // 2, x, own_part, :] = predicted
+                if f == 0:
+                    YP[0, x, own_part, :] = predicted
 
         planes(0, BX, 2, predict)
+        a2_left_p.start()
+        a2_right_p.start()
+        exchange(a2_low[0], a2_high[0], "start")
+
+        def take_source(f, x, total):
+            at = pl.ds(pl.multiple_of((x + H) * BY, BY), BY)
+            predicted = state_p[f + 1, at, :] - ape_time_step * total
+            state_p[f + 1, at, :] = predicted
+            if f == 1:
+                YP[1, x, own_part, :] = predicted
+
+        deposit(LB, True, take_source)
         a2_left.start()
         a2_right.start()
-        for low, high in zip(a2_low, a2_high):
-            exchange(low, high, "start")
-
+        exchange(a2_low[1], a2_high[1], "start")
+        pack(ahead, 1, BX, WL, WH, 0, 3)
+        exchange(*late_pred, "start")
+
+        rate_z(state_p)
         exchange(edge_pred[1], edge_pred[0], "wait_recv")
-        planes(4, 44, 2, second_lamb)
-        deposit()
+        planes(BX + 2, BX + 28, 2, second_lamb)
+        deposit(LC, False, keep_in(E))
         for low, high in zip(a2_low, a2_high):
             exchange(high, low, "wait_recv")
-        rate_yz(state_p, YP)
-        a2_left.wait_recv()
-        a2_right.wait_recv()
+        rate_y(YP)
+
+        def more_source(f, x, total):
+            to = pl.ds(pl.multiple_of(x * BY, BY), BY)
+            E[f, to, :] = E[f, to, :] + total
+
+        exchange(late_pred[1], late_pred[0], "wait_recv")
+        planes(4, BX + 2, 2, second_lamb)
+        deposit(LC, True, more_source)
+        for c in (a2_left_p, a2_right_p, a2_left, a2_right):
+            c.wait_recv()
 
         def correct(x):
             tend = rate_x(state_p, x)
             at = pl.ds(pl.multiple_of((x + H) * BY, BY), BY)
             to = pl.ds(pl.multiple_of(x * BY, BY), BY)
             for f in range(4):
-                t = tend[f] - dep[f - 1, to, :] if f else tend[f]
+                t = tend[f] - E[f - 1, to, :] if f else tend[f]
                 final[f, to, :] = 0.5 * (
                     state[f, at, :] + state_p[f, at, :] + ape_time_step * t
                 )
 
         planes(0, BX, 2, correct)
-        here(L_OUT, O, out).start()
-        for c in tables + [relay_hi, relay_lo, a1_left, a1_right, a2_left, a2_right]:
+        for c in tables + relays + [a1_left, a1_right, a2_left, a2_right]:
             c.wait_send()
-        for pair in (edge_own, edge_next, edge_prev, edge_pred):
+        for c in (a2_left_p, a2_right_p):
+            c.wait_send()
+        for pair in (edge_prev, edge_pred, late_pred):
             exchange(*pair, "wait_send")
         for lows, highs in ((a1_low, a1_high), (a2_low, a2_high)):
             for low, high in zip(lows, highs):
                 exchange(low, high, "wait_send")
-        here(L_OUT, O, out).wait()
 
 
 def on_device(flow_state, block_offset, block_weight):
@@ -549,31 +641,32 @@
         planes_of(4, BX + 2 * H),
         vmem(2, BX, 3 * BY, NZ),
         planes_of(3, 3 * BX),
+        *[vmem(3, 3 * BX, NZ)] * 2,
+        planes_of(3, 3 * BX),
         *[vmem(3, 3 * BX, NZ)] * 4,
         planes_of(3, 3 * BX),
-        *[vmem(3, 3 * BX, NZ)] * 4,
         planes_of(3, 3 * BX),
         planes_of(4, BX),
         planes_of(4, BX + 2 * H),
         vmem(2, BX, 3 * BY, NZ),
         planes_of(3, BX),
+        planes_of(3, BX),
         vmem(3, BY, NZ),
         vmem(25, BY, NZ),
-        planes_of(4, BX),
         pltpu.SMEM((NB,), jnp.int32),
         pltpu.SMEM((NB,), f32),
         pltpu.SemaphoreType.DMA((N_REMOTE,)),
         pltpu.SemaphoreType.DMA((N_REMOTE,)),
         pltpu.SemaphoreType.DMA((N_LOCAL,)),
     ]
-    anywhere = pl.BlockSpec(memory_space=pl.ANY)
+    anywhere = pl.BlockSpec(memory_space=pltpu.HBM)
     advanced = pl.pallas_call(
         functools.partial(kernel, gx_size, gy_size),
         out_shape=jax.ShapeDtypeStruct((4, BX * BY, NZ), f32),
         in_specs=[anywhere] * 4,
-        out_specs=anywhere,
+        out_specs=pl.BlockSpec(memory_space=pltpu.VMEM),
         scratch_shapes=scratch,
-        compiler_params=pltpu.CompilerParams(collective_id=0, has_side_effects=True),
+        compiler_params=pltpu.CompilerParams(collective_id=0, has_side_effects=True, vmem_limit_bytes=56250000),
         name="heun",
     )(flow_state.reshape(4, BX * BY, NZ), flow_state[0], block_offset, block_weight)
     return advanced.reshape(flow_state.shape)

time: 40.4 us -> 36.8 us (0.911)
  the two profiles are of different devices: /device:TPU:66 before, /device:TPU:67 now
where the time goes in v2:
time: 36.8 us; the launch traced here: 36.6 us
  Pallas kernels  35.3 us (96%)
  local copies, waits for them, and re-layouts  1.37 us (4%)
    pallas_call x1, Pallas kernels, on_device(): pl.pallas_call(functools.partial(kernel, gx_size, gy_size), out_shape=jax...  35.3 us
    unnamed x5, local copies, waits for them, and re-layouts  1.37 us

profile of v2, /device:TPU:67, one launch (start us, length us, event | category | flops | bytes accessed | tf_op | source)
XLA Modules:
  0.0 36.6 jit_solution(446438983143426110)
XLA Ops:
  0.0 0.0 copy-start
  0.0 0.0 copy-start.1
  0.0 0.7 %copy-done = s32[4]{0:T(128)S(1)} copy-done((s32[4]{0:T(128)S(1)}, s32[4]{0:T(128)}, u32[]{:S(2)}) %copy-start) | copy-done | bytes 40
  0.7 0.0 copy-done.1
  0.7 35.3 %heun.1 = f32[4,128,128]{2,1,0:T(8,128)S(1)} custom-call(f32[4,128,128]{2,1,0:T(8,128)} %bitcast.4, f32[4,16,8,128]{3,2,1,0:T(8,128)} %bitcast.5, s32[4]{0:T(128)S(1)} %copy-done, f32[4]{0:T(128)S(1)} %copy-done.1), custom_call_target="tpu_custom_call" | custom-call | tf_op jit(solution)/shard_map/heun/pallas_call | solution.py:663
  35.9 0.7 %copy.5 = f32[1,4,16,8,128]{4,3,2,1,0:T(8,128)} copy(f32[1,4,16,8,128]{4,3,2,1,0:T(8,128)S(1)} %bitcast.3) | data formatting | bytes 524288
Async XLA Ops:
  0.0 0.7 %copy-start = (s32[4]{0:T(128)S(1)}, s32[4]{0:T(128)}, u32[]{:S(2)}) copy-start(s32[4]{0:T(128)} %offset.1) | copy-start | bytes 52
  0.0 0.7 %copy-start.1 = (f32[4]{0:T(128)S(1)}, f32[4]{0:T(128)}, u32[]{:S(2)}) copy-start(f32[4]{0:T(128)} %weight.1) | copy-start | bytes 52

commit v3 on v2

--- a/solution.py
+++ b/solution.py
@@ -33,12 +33,13 @@
 (
     LES_XL, LES_XR, LES_YL, LES_YH,
     PRED_XL, PRED_XR, PRED_YL, PRED_YH,
-    RAW_0, RAW_1, RAW_2, RAW_3, RAW_NEXT,
-    RELAY_0, RELAY_1, RELAY_2, RELAY_3,
+    RAW_0, RAW_1, RAW_NEXT,
+    RELAY_0, RELAY_1,
     TAB_L, TAB_R,
     A1_XL, A1_XR, A1_YLP, A1_YLV, A1_YHP, A1_YHV,
     A2_XL, A2_XR, A2_XLP, A2_XRP, A2_YLP, A2_YLV, A2_YHP, A2_YHV,
-    EDGE_OWN_L, EDGE_OWN_H, EDGE_NEXT_L, EDGE_NEXT_H, EDGE_PREV_L, EDGE_PREV_H,
+    EDGE_NEXT_L, EDGE_NEXT_H,
+    OWN_1_L, OWN_1_H, OWN_2_L, OWN_2_H, PREV_1_L, PREV_1_H, PREV_2_L, PREV_2_H,
     EDGE_P_L, EDGE_P_H, LATE_P_L, LATE_P_H,
     N_REMOTE,
 ) = range(44)
@@ -116,7 +117,7 @@
     gx_size, gy_size,
     flow, flow_planes, offset, weight, out,
     X, XL, XH, EL, EH, XP, PL, PH, QL, QH,
-    F, YE, R, RL, RH, V, VL, VH, WL, WH, LB, LC, G, FP, YP, D, E, TAB, COEF,
+    F, YE, R, RL, RH, SL, SH, V, VL, VH, WL, WH, LB, LC, G, FP, YP, E, TAB, COEF,
     off_s, wt_s, send_sem, recv_sem, local_sem,
 ):
     grp, gx, gy = lax.axis_index("grp"), lax.axis_index("gx"), lax.axis_index("gy")
@@ -145,7 +146,7 @@
         copy(LES_XL, flow.at[:, cells_of(0, 1)], X.at[:, cells_of(BX + 1, 1)], me_left),
         copy(LES_XR, flow.at[:, cells_of(BX - 1, 1)], X.at[:, cells_of(0, 1)], me_right),
     ]
-    pieces = [(12, 4), (8, 4), (4, 4), (0, 4)]
+    pieces = [(3, 13), (0, 3)]
     velocity = pl.ds(0, 3)
     les_raw = [
         copy(
@@ -211,18 +212,20 @@
     ]
     third = [pl.ds(0, BX), pl.ds(BX, BX), pl.ds(2 * BX, BX)]
 
-    edge_own = (
-        copy(EDGE_OWN_L, EL.at[velocity], RH.at[:, third[1]], (1, gx, gy - 1)),
-        copy(EDGE_OWN_H, EH.at[velocity], RL.at[:, third[1]], (1, gx, gy + 1)),
-    )
     edge_next = (
         copy(EDGE_NEXT_L, EL.at[velocity], RH.at[:, third[2]], (1, left, gy - 1)),
         copy(EDGE_NEXT_H, EH.at[velocity], RL.at[:, third[2]], (1, left, gy + 1)),
     )
-    edge_prev = (
-        copy(EDGE_PREV_L, RL.at[:, third[1]], RL.at[:, third[0]], me_right),
-        copy(EDGE_PREV_H, RH.at[:, third[1]], RH.at[:, third[0]], me_right),
-    )
+
+    def edges(kind, first):
+        part = pl.ds(first, 8)
+        return (
+            copy(kind, SL.at[:, part], RH.at[:, part], me_low),
+            copy(kind + 1, SH.at[:, part], RL.at[:, part], me_high),
+        )
+
+    edge_own_1, edge_own_2 = edges(OWN_1_L, BX + 8), edges(OWN_2_L, BX)
+    edge_prev_1, edge_prev_2 = edges(PREV_1_L, 8), edges(PREV_2_L, 0)
     soon, late = pl.ds(BX, 2 * BX), pl.ds(0, BX)
     edge_pred = (
         copy(EDGE_P_L, WL.at[:, soon], VH.at[:, soon], me_low),
@@ -260,12 +263,10 @@
 
         @pl.when(has_low)
         def _():
-            greet((1, gx, gy - 1))
             greet((1, left, gy - 1))
 
         @pl.when(has_high)
         def _():
-            greet((1, gx, gy + 1))
             greet((1, left, gy + 1))
 
     @pl.when(is_ape)
@@ -274,12 +275,10 @@
 
         @pl.when(has_low)
         def _():
-            greet((0, gx, gy - 1))
             greet((0, right, gy - 1))
 
         @pl.when(has_high)
         def _():
-            greet((0, gx, gy + 1))
             greet((0, right, gy + 1))
 
     @pl.when(has_low)
@@ -339,10 +338,9 @@
         cells, ahead, final = X, XP, out
         here(L_FLOW, flow, X.at[:, cells_of(1, BX)]).wait()
         pack(cells, 1, BX, EL, EH, 0, 4)
-        pl.semaphore_wait(barrier, 4 + 3 * y_neighbours)
-        exchange(*edge_own, "start")
+        pl.semaphore_wait(barrier, 4 + 2 * y_neighbours)
         exchange(*edge_next, "start")
-        for c in les_raw + [les_next] + les_first:
+        for c in les_raw[:1] + [les_next] + les_first + les_raw[1:]:
             c.start()
         exchange(les_edge_low, les_edge_high, "start")
         for c in les_first:
@@ -380,7 +378,6 @@
             c.wait_send()
         exchange(les_edge_low, les_edge_high, "wait_send")
         exchange(pred_low, pred_high, "wait_send")
-        exchange(*edge_own, "wait_send")
         exchange(*edge_next, "wait_send")
 
     @pl.when(is_ape)
@@ -396,10 +393,9 @@
             table = jnp.where(sub == NB + b, wt_s[b], table)
         TAB[1] = table
 
-        pl.semaphore_wait(barrier, 4 + 3 * y_neighbours)
+        pl.semaphore_wait(barrier, 4 + 2 * y_neighbours)
         for c in tables:
             c.start()
-        a1_right.start()
         a1_left.start()
         for low, high in zip(a1_low, a1_high):
             exchange(low, high, "start")
@@ -512,24 +508,20 @@
 
             return add
 
-        exchange(edge_own[1], edge_own[0], "wait_recv")
-        exchange(*edge_prev, "start")
-        for k in range(2):
-            les_raw[k].wait_recv()
-            relays[k].start()
-        planes(BX + 9, BX + 15, 2, first_lamb)
-        les_raw[2].wait_recv()
-        relays[2].start()
-        planes(BX + 5, BX + 9, 2, first_lamb)
-        les_raw[3].wait_recv()
-        relays[3].start()
-        planes(BX + 1, BX + 5, 2, first_lamb)
+        les_raw[0].wait_recv()
+        relays[0].start()
+        a1_right.start()
+        pack(raw, BX + 8, 8, SL, SH, BX + 8, 3)
+        exchange(*edge_own_1, "start")
+        les_raw[1].wait_recv()
+        relays[1].start()
+        pack(raw, BX, 8, SL, SH, BX, 3)
+        exchange(*edge_own_2, "start")
 
         exchange(edge_next[1], edge_next[0], "wait_recv")
         les_next.wait_recv()
-        planes(2 * BX - 1, 2 * BX + 13, 2, first_lamb)
-        pack(ahead, BX + 1, 28, WL, WH, BX, 3)
-        exchange(*edge_pred, "start")
+        exchange(edge_own_1[1], edge_own_1[0], "wait_recv")
+        planes(BX + 9, 2 * BX + 13, 2, first_lamb)
         for c in tables:
             c.wait_recv()
         for k, (d, part, b, aim) in enumerate(pairs):
@@ -538,7 +530,6 @@
             COEF[k] = jnp.where(target == float(aim), share, 0.0) + jnp.where(
                 target + 1.0 == float(aim), 1.0 - share, 0.0
             )
-        deposit(LB, False, keep_in(D))
 
         here(L_YP, flow_planes.at[0], YE.at[0, :, own_part]).wait()
         here(L_YV, flow_planes.at[2], YE.at[1, :, own_part]).wait()
@@ -546,10 +537,11 @@
             exchange(high, low, "wait_recv")
         rate_y(YE)
 
-        exchange(*edge_prev, "wait_recv")
-        for k, (first, last) in enumerate(((13, 17), (9, 13), (5, 9), (3, 5))):
-            relays[k].wait_recv()
-            planes(first, last, 2, first_lamb)
+        relays[0].wait_recv()
+        pack(raw, 8, 8, SL, SH, 8, 3)
+        exchange(*edge_prev_1, "start")
+        pack(raw, 3, 5, SL, SH, 3, 3)
+        exchange(*edge_prev_2, "start")
 
         a1_left.wait_recv()
         a1_right.wait_recv()
@@ -557,10 +549,8 @@
         def predict(x):
             tend = rate_x(state, x)
             at = pl.ds(pl.multiple_of((x + H) * BY, BY), BY)
-            to = pl.ds(pl.multiple_of(x * BY, BY), BY)
             for f in range(4):
-                t = tend[f] - D[f - 1, to, :] if f else tend[f]
-                predicted = state[f, at, :] + ape_time_step * t
+                predicted = state[f, at, :] + ape_time_step * tend[f]
                 state_p[f, at, :] = predicted
                 if f == 0:
                     YP[0, x, own_part, :] = predicted
@@ -569,6 +559,22 @@
         a2_left_p.start()
         a2_right_p.start()
         exchange(a2_low[0], a2_high[0], "start")
+
+        def take_part(f, x, total):
+            at = pl.ds(pl.multiple_of((x + H) * BY, BY), BY)
+            state_p[f + 1, at, :] = state_p[f + 1, at, :] - ape_time_step * total
+
+        exchange(edge_own_2[1], edge_own_2[0], "wait_recv")
+        planes(BX + 1, BX + 9, 2, first_lamb)
+        pack(ahead, BX + 1, 28, WL, WH, BX, 3)
+        exchange(*edge_pred, "start")
+        deposit(LB, False, take_part)
+
+        exchange(edge_prev_1[1], edge_prev_1[0], "wait_recv")
+        planes(9, BX + 1, 2, first_lamb)
+        exchange(edge_prev_2[1], edge_prev_2[0], "wait_recv")
+        planes(4, 8, 2, first_lamb)
+        planes(8, 9, 1, first_lamb)
 
         def take_source(f, x, total):
             at = pl.ds(pl.multiple_of((x + H) * BY, BY), BY)
@@ -583,6 +589,8 @@
         exchange(a2_low[1], a2_high[1], "start")
         pack(ahead, 1, BX, WL, WH, 0, 3)
         exchange(*late_pred, "start")
+        relays[1].wait_recv()
+        planes(3, 4, 1, first_lamb)
 
         rate_z(state_p)
         exchange(edge_pred[1], edge_pred[0], "wait_recv")
@@ -617,7 +625,7 @@
             c.wait_send()
         for c in (a2_left_p, a2_right_p):
             c.wait_send()
-        for pair in (edge_prev, edge_pred, late_pred):
+        for pair in (edge_own_1, edge_own_2, edge_prev_1, edge_prev_2, edge_pred, late_pred):
             exchange(*pair, "wait_send")
         for lows, highs in ((a1_low, a1_high), (a2_low, a2_high)):
             for low, high in zip(lows, highs):
@@ -642,6 +650,7 @@
         vmem(2, BX, 3 * BY, NZ),
         planes_of(3, 3 * BX),
         *[vmem(3, 3 * BX, NZ)] * 2,
+        *[vmem(3, 2 * BX, NZ)] * 2,
         planes_of(3, 3 * BX),
         *[vmem(3, 3 * BX, NZ)] * 4,
         planes_of(3, 3 * BX),
@@ -649,7 +658,6 @@
         planes_of(4, BX),
         planes_of(4, BX + 2 * H),
         vmem(2, BX, 3 * BY, NZ),
-        planes_of(3, BX),
         planes_of(3, BX),
         vmem(3, BY, NZ),
         vmem(25, BY, NZ),

time: 36.8 us -> 34.9 us (0.948)
  the two profiles are of different devices: /device:TPU:67 before, /device:TPU:69 now
where the time goes in v3:
time: 34.9 us; the launch traced here: 34.8 us
  Pallas kernels  33.4 us (96%)
  local copies, waits for them, and re-layouts  1.37 us (4%)
    pallas_call x1, Pallas kernels, on_device(): pl.pallas_call(functools.partial(kernel, gx_size, gy_size), out_shape=jax...  33.4 us
    unnamed x5, local copies, waits for them, and re-layouts  1.37 us

profile of v3, /device:TPU:69, one launch (start us, length us, event | category | flops | bytes accessed | tf_op | source)
XLA Modules:
  0.0 34.8 jit_solution(2240824998224849955)
XLA Ops:
  0.0 0.0 copy-start
  0.0 0.0 copy-start.1
  0.0 0.7 %copy-done = s32[4]{0:T(128)S(1)} copy-done((s32[4]{0:T(128)S(1)}, s32[4]{0:T(128)}, u32[]{:S(2)}) %copy-start) | copy-done | bytes 40
  0.7 0.0 copy-done.1
  0.7 33.4 %heun.1 = f32[4,128,128]{2,1,0:T(8,128)S(1)} custom-call(f32[4,128,128]{2,1,0:T(8,128)} %bitcast.4, f32[4,16,8,128]{3,2,1,0:T(8,128)} %bitcast.5, s32[4]{0:T(128)S(1)} %copy-done, f32[4]{0:T(128)S(1)} %copy-done.1), custom_call_target="tpu_custom_call" | custom-call | tf_op jit(solution)/shard_map/heun/pallas_call | solution.py:671
  34.1 0.7 %copy.5 = f32[1,4,16,8,128]{4,3,2,1,0:T(8,128)} copy(f32[1,4,16,8,128]{4,3,2,1,0:T(8,128)S(1)} %bitcast.3) | data formatting | bytes 524288
Async XLA Ops:
  0.0 0.7 %copy-start = (s32[4]{0:T(128)S(1)}, s32[4]{0:T(128)}, u32[]{:S(2)}) copy-start(s32[4]{0:T(128)} %offset.1) | copy-start | bytes 52
  0.0 0.7 %copy-start.1 = (f32[4]{0:T(128)S(1)}, f32[4]{0:T(128)}, u32[]{:S(2)}) copy-start(f32[4]{0:T(128)} %weight.1) | copy-start | bytes 52

commit v4 on v3

--- a/solution.py
+++ b/solution.py
@@ -117,7 +117,7 @@
     gx_size, gy_size,
     flow, flow_planes, offset, weight, out,
     X, XL, XH, EL, EH, XP, PL, PH, QL, QH,
-    F, YE, R, RL, RH, SL, SH, V, VL, VH, WL, WH, LB, LC, G, FP, YP, E, TAB, COEF,
+    F, YE, R, RL, RH, SL, SH, V, VL, VH, WL, WH, LB, LC, G, FP, YP, D, E, TAB, COEF,
     off_s, wt_s, send_sem, recv_sem, local_sem,
 ):
     grp, gx, gy = lax.axis_index("grp"), lax.axis_index("gx"), lax.axis_index("gy")
@@ -125,6 +125,7 @@
     left = lax.rem(gx + gx_size - 1, gx_size)
     has_low, has_high = gy > 0, gy < gy_size - 1
     is_les, is_ape = grp == 0, grp == 1
+    place = lax.rem(gx, 4)
 
     def copy(kind, src, dst, device):
         return pltpu.make_async_remote_copy(
@@ -396,7 +397,16 @@
         pl.semaphore_wait(barrier, 4 + 2 * y_neighbours)
         for c in tables:
             c.start()
-        a1_left.start()
+
+        @pl.when((place == 0))
+        def _():
+            a1_right.start()
+
+
+        @pl.when((place == 1) | (place == 2) | (place == 3))
+        def _():
+            a1_left.start()
+
         for low, high in zip(a1_low, a1_high):
             exchange(low, high, "start")
 
@@ -510,7 +520,16 @@
 
         les_raw[0].wait_recv()
         relays[0].start()
-        a1_right.start()
+
+        @pl.when((place == 0))
+        def _():
+            a1_left.start()
+
+
+        @pl.when((place == 1) | (place == 3))
+        def _():
+            a1_right.start()
+
         pack(raw, BX + 8, 8, SL, SH, BX + 8, 3)
         exchange(*edge_own_1, "start")
         les_raw[1].wait_recv()
@@ -520,6 +539,11 @@
 
         exchange(edge_next[1], edge_next[0], "wait_recv")
         les_next.wait_recv()
+
+        @pl.when((place == 2))
+        def _():
+            a1_right.start()
+
         exchange(edge_own_1[1], edge_own_1[0], "wait_recv")
         planes(BX + 9, 2 * BX + 13, 2, first_lamb)
         for c in tables:
@@ -543,14 +567,22 @@
         pack(raw, 3, 5, SL, SH, 3, 3)
         exchange(*edge_prev_2, "start")
 
+        exchange(edge_own_2[1], edge_own_2[0], "wait_recv")
+        planes(BX + 1, BX + 9, 2, first_lamb)
+        pack(ahead, BX + 1, 28, WL, WH, BX, 3)
+        exchange(*edge_pred, "start")
+        deposit(LB, False, keep_in(D))
+
         a1_left.wait_recv()
         a1_right.wait_recv()
 
         def predict(x):
             tend = rate_x(state, x)
             at = pl.ds(pl.multiple_of((x + H) * BY, BY), BY)
+            to = pl.ds(pl.multiple_of(x * BY, BY), BY)
             for f in range(4):
-                predicted = state[f, at, :] + ape_time_step * tend[f]
+                t = tend[f] - D[f - 1, to, :] if f else tend[f]
+                predicted = state[f, at, :] + ape_time_step * t
                 state_p[f, at, :] = predicted
                 if f == 0:
                     YP[0, x, own_part, :] = predicted
@@ -559,16 +591,6 @@
         a2_left_p.start()
         a2_right_p.start()
         exchange(a2_low[0], a2_high[0], "start")
-
-        def take_part(f, x, total):
-            at = pl.ds(pl.multiple_of((x + H) * BY, BY), BY)
-            state_p[f + 1, at, :] = state_p[f + 1, at, :] - ape_time_step * total
-
-        exchange(edge_own_2[1], edge_own_2[0], "wait_recv")
-        planes(BX + 1, BX + 9, 2, first_lamb)
-        pack(ahead, BX + 1, 28, WL, WH, BX, 3)
-        exchange(*edge_pred, "start")
-        deposit(LB, False, take_part)
 
         exchange(edge_prev_1[1], edge_prev_1[0], "wait_recv")
         planes(9, BX + 1, 2, first_lamb)
@@ -659,6 +681,7 @@
         planes_of(4, BX + 2 * H),
         vmem(2, BX, 3 * BY, NZ),
         planes_of(3, BX),
+        planes_of(3, BX),
         vmem(3, BY, NZ),
         vmem(25, BY, NZ),
         pltpu.SMEM((NB,), jnp.int32),

time: 34.9 us -> 33.9 us (0.971)
  the two profiles are of different devices: /device:TPU:69 before, /device:TPU:64 now
where the time goes in v4:
time: 33.9 us; the launch traced here: 33.8 us
  Pallas kernels  32.4 us (96%)
  local copies, waits for them, and re-layouts  1.37 us (4%)
    pallas_call x1, Pallas kernels, on_device(): pl.pallas_call(functools.partial(kernel, gx_size, gy_size), out_shape=jax...  32.4 us
    unnamed x5, local copies, waits for them, and re-layouts  1.37 us

profile of v4, /device:TPU:64, one launch (start us, length us, event | category | flops | bytes accessed | tf_op | source)
XLA Modules:
  0.0 33.8 jit_solution(5802732052897178816)
XLA Ops:
  0.0 0.0 copy-start
  0.0 0.0 copy-start.1
  0.0 0.7 %copy-done = s32[4]{0:T(128)S(1)} copy-done((s32[4]{0:T(128)S(1)}, s32[4]{0:T(128)}, u32[]{:S(2)}) %copy-start) | copy-done | bytes 40
  0.7 0.0 copy-done.1
  0.7 32.4 %heun.1 = f32[4,128,128]{2,1,0:T(8,128)S(1)} custom-call(f32[4,128,128]{2,1,0:T(8,128)} %bitcast.4, f32[4,16,8,128]{3,2,1,0:T(8,128)} %bitcast.5, s32[4]{0:T(128)S(1)} %copy-done, f32[4]{0:T(128)S(1)} %copy-done.1), custom_call_target="tpu_custom_call" | custom-call | tf_op jit(solution)/shard_map/heun/pallas_call | solution.py:694
  33.1 0.7 %copy.5 = f32[1,4,16,8,128]{4,3,2,1,0:T(8,128)} copy(f32[1,4,16,8,128]{4,3,2,1,0:T(8,128)S(1)} %bitcast.3) | data formatting | bytes 524288
Async XLA Ops:
  0.0 0.7 %copy-start = (s32[4]{0:T(128)S(1)}, s32[4]{0:T(128)}, u32[]{:S(2)}) copy-start(s32[4]{0:T(128)} %offset.1) | copy-start | bytes 52
  0.0 0.7 %copy-start.1 = (f32[4]{0:T(128)S(1)}, f32[4]{0:T(128)}, u32[]{:S(2)}) copy-start(f32[4]{0:T(128)} %weight.1) | copy-start | bytes 52

commit v5 on v4

--- a/solution.py
+++ b/solution.py
@@ -33,8 +33,8 @@
 (
     LES_XL, LES_XR, LES_YL, LES_YH,
     PRED_XL, PRED_XR, PRED_YL, PRED_YH,
-    RAW_0, RAW_1, RAW_NEXT,
-    RELAY_0, RELAY_1,
+    RAW_0, RAW_1, RAW_2, RAW_NEXT,
+    RELAY_0, RELAY_1, RELAY_2,
     TAB_L, TAB_R,
     A1_XL, A1_XR, A1_YLP, A1_YLV, A1_YHP, A1_YHV,
     A2_XL, A2_XR, A2_XLP, A2_XRP, A2_YLP, A2_YLV, A2_YHP, A2_YHV,
@@ -42,7 +42,7 @@
     OWN_1_L, OWN_1_H, OWN_2_L, OWN_2_H, PREV_1_L, PREV_1_H, PREV_2_L, PREV_2_H,
     EDGE_P_L, EDGE_P_H, LATE_P_L, LATE_P_H,
     N_REMOTE,
-) = range(44)
+) = range(46)
 L_FLOW, L_YP, L_YV, L_OFF, L_WT, L_OUT, N_LOCAL = range(7)
 
 
@@ -147,7 +147,7 @@
         copy(LES_XL, flow.at[:, cells_of(0, 1)], X.at[:, cells_of(BX + 1, 1)], me_left),
         copy(LES_XR, flow.at[:, cells_of(BX - 1, 1)], X.at[:, cells_of(0, 1)], me_right),
     ]
-    pieces = [(3, 13), (0, 3)]
+    pieces = [(8, 8), (3, 5), (0, 3)]
     velocity = pl.ds(0, 3)
     les_raw = [
         copy(
@@ -341,7 +341,7 @@
         pack(cells, 1, BX, EL, EH, 0, 4)
         pl.semaphore_wait(barrier, 4 + 2 * y_neighbours)
         exchange(*edge_next, "start")
-        for c in les_raw[:1] + [les_next] + les_first + les_raw[1:]:
+        for c in les_raw[:2] + [les_next] + les_first + les_raw[2:]:
             c.start()
         exchange(les_edge_low, les_edge_high, "start")
         for c in les_first:
@@ -519,7 +519,9 @@
             return add
 
         les_raw[0].wait_recv()
+        les_raw[1].wait_recv()
         relays[0].start()
+        relays[1].start()
 
         @pl.when((place == 0))
         def _():
@@ -532,8 +534,8 @@
 
         pack(raw, BX + 8, 8, SL, SH, BX + 8, 3)
         exchange(*edge_own_1, "start")
-        les_raw[1].wait_recv()
-        relays[1].start()
+        les_raw[2].wait_recv()
+        relays[2].start()
         pack(raw, BX, 8, SL, SH, BX, 3)
         exchange(*edge_own_2, "start")
 
@@ -564,11 +566,12 @@
         relays[0].wait_recv()
         pack(raw, 8, 8, SL, SH, 8, 3)
         exchange(*edge_prev_1, "start")
+        relays[1].wait_recv()
         pack(raw, 3, 5, SL, SH, 3, 3)
         exchange(*edge_prev_2, "start")
 
         exchange(edge_own_2[1], edge_own_2[0], "wait_recv")
-        planes(BX + 1, BX + 9, 2, first_lamb)
+        planes(BX + 1, BX + 9, 4, first_lamb)
         pack(ahead, BX + 1, 28, WL, WH, BX, 3)
         exchange(*edge_pred, "start")
         deposit(LB, False, keep_in(D))
@@ -587,15 +590,15 @@
                 if f == 0:
                     YP[0, x, own_part, :] = predicted
 
-        planes(0, BX, 2, predict)
+        planes(0, BX, 4, predict)
         a2_left_p.start()
         a2_right_p.start()
         exchange(a2_low[0], a2_high[0], "start")
 
         exchange(edge_prev_1[1], edge_prev_1[0], "wait_recv")
-        planes(9, BX + 1, 2, first_lamb)
+        planes(9, BX + 1, 4, first_lamb)
         exchange(edge_prev_2[1], edge_prev_2[0], "wait_recv")
-        planes(4, 8, 2, first_lamb)
+        planes(4, 8, 4, first_lamb)
         planes(8, 9, 1, first_lamb)
 
         def take_source(f, x, total):
@@ -611,7 +614,7 @@
         exchange(a2_low[1], a2_high[1], "start")
         pack(ahead, 1, BX, WL, WH, 0, 3)
         exchange(*late_pred, "start")
-        relays[1].wait_recv()
+        relays[2].wait_recv()
         planes(3, 4, 1, first_lamb)
 
         rate_z(state_p)
@@ -642,7 +645,7 @@
                     state[f, at, :] + state_p[f, at, :] + ape_time_step * t
                 )
 
-        planes(0, BX, 2, correct)
+        planes(0, BX, 4, correct)
         for c in tables + relays + [a1_left, a1_right, a2_left, a2_right]:
             c.wait_send()
         for c in (a2_left_p, a2_right_p):

time: 33.9 us -> 33.7 us (level)
  no operation moved by 1% of the time
where the time goes in v5:
time: 33.7 us; the launch traced here: 33.5 us
  Pallas kernels  32.1 us (95%)
  local copies, waits for them, and re-layouts  1.37 us (4%)
    pallas_call x1, Pallas kernels, on_device(): pl.pallas_call(functools.partial(kernel, gx_size, gy_size), out_shape=jax...  32.1 us
    unnamed x5, local copies, waits for them, and re-layouts  1.37 us

profile of v5, /device:TPU:64, one launch (start us, length us, event | category | flops | bytes accessed | tf_op | source)
XLA Modules:
  0.0 33.5 jit_solution(17910443376371803658)
XLA Ops:
  0.0 0.0 copy-start
  0.0 0.0 copy-start.1
  0.0 0.7 %copy-done = s32[4]{0:T(128)S(1)} copy-done((s32[4]{0:T(128)S(1)}, s32[4]{0:T(128)}, u32[]{:S(2)}) %copy-start) | copy-done | bytes 40
  0.7 0.0 copy-done.1
  0.7 32.1 %heun.1 = f32[4,128,128]{2,1,0:T(8,128)S(1)} custom-call(f32[4,128,128]{2,1,0:T(8,128)} %bitcast.4, f32[4,16,8,128]{3,2,1,0:T(8,128)} %bitcast.5, s32[4]{0:T(128)S(1)} %copy-done, f32[4]{0:T(128)S(1)} %copy-done.1), custom_call_target="tpu_custom_call" | custom-call | tf_op jit(solution)/shard_map/heun/pallas_call | solution.py:697
  32.7 0.7 %copy.5 = f32[1,4,16,8,128]{4,3,2,1,0:T(8,128)} copy(f32[1,4,16,8,128]{4,3,2,1,0:T(8,128)S(1)} %bitcast.3) | data formatting | bytes 524288
Async XLA Ops:
  0.0 0.7 %copy-start = (s32[4]{0:T(128)S(1)}, s32[4]{0:T(128)}, u32[]{:S(2)}) copy-start(s32[4]{0:T(128)} %offset.1) | copy-start | bytes 52
  0.0 0.7 %copy-start.1 = (f32[4]{0:T(128)S(1)}, f32[4]{0:T(128)}, u32[]{:S(2)}) copy-start(f32[4]{0:T(128)} %weight.1) | copy-start | bytes 52
